TPU v7x, 32 devices: a whole 2x2x4 slice. The times are simulated.
32 devices in a mesh: groups: 2 (over y), site: 4 (over z), member: 4 (over x, core).
Axes of the slice: x: 2, y: 2, z: 4, core: 2. Of those that a mesh axis runs over, the one named last changes fastest.
Arguments:
- tokens: bfloat16 [2048, 2880], P(('groups', 'site', 'member')), parts along dimension 0, may hold values from -6 to 6
- expert_ids: int32 [2048, 4], P(('groups', 'site', 'member')), parts along dimension 0, may hold values from 0 to 15, as said below
- route_weights: bfloat16 [2048, 4], P(('groups', 'site', 'member')), parts along dimension 0, may hold values from 0.049804688 to 1
- w_gate: bfloat16 [16, 2880, 2880], P(('site', 'member')), may hold values from -0.109375 to 0.109375
- w_up: bfloat16 [16, 2880, 2880], P(('site', 'member')), may hold values from -0.109375 to 0.109375
- w_down: bfloat16 [16, 2880, 2880], P(('site', 'member')), may hold values from -0.109375 to 0.109375
Outputs:
- mixed: bfloat16 [2048, 2880], P(('groups', 'site', 'member')), parts along dimension 0
There are 2 independent parts, one for each index of `groups`. A program takes and returns all parts, laid end to end along the dimension named above; an argument that names none is the same for every part. Nothing has to cross between parts.
Inputs may be any that keep to these rules, and one draw needn't show every extreme that they name: `expert_ids`: each row names 4 different experts. At most 18 of the 64 tokens of one device name any one expert.
All inputs are finite; a program needn't handle non-finite values.
Results may differ from a plain program's by a relative error of at most 0.014.
Values may be sent and summed in bfloat16 or wider, within the bound.
No kernel may reach another device: no remote copies, remote signals or barrier semaphores. Data moves between devices by JAX's collectives and lax.ppermute only.
A program may use at most 192 MiB of HBM per device.

v0:
```python
import jax
import jax.numpy as jnp
from jax import lax
from jax.sharding import PartitionSpec as P

EXP_SITE = 4


alpha_glu = 1.702


def weight_table(expert_ids, route_weights, experts):
    columns = lax.broadcasted_iota(jnp.int32, (1, 1, experts), 2)
    matches = expert_ids[:, :, None] == columns
    spread = jnp.where(matches, route_weights[:, :, None].astype(jnp.float32), 0.0)
    return jnp.sum(spread, axis=1).astype(jnp.bfloat16)


def pack_rows(inputs, needed, capacity):
    position = jnp.cumsum(needed.astype(jnp.int32), axis=0) - 1
    target = jnp.where(needed, position, capacity)
    group_ids = lax.broadcasted_iota(jnp.int32, needed.shape, 1)
    packed = jnp.zeros((needed.shape[1], capacity, inputs.shape[1]), inputs.dtype)
    spread_rows = jnp.broadcast_to(inputs[:, None, :], needed.shape + (inputs.shape[1],))
    packed = packed.at[group_ids, target].set(spread_rows, mode="drop")
    return (packed, jnp.minimum(target, capacity - 1), group_ids)


def expert_apply(received, gate_weight, up_weight, down_weight):
    feature_width = received.shape[-1]
    flat_rows = received.reshape(-1, feature_width)
    gate_value = jnp.dot(flat_rows, gate_weight, preferred_element_type=jnp.float32)
    up_value = jnp.dot(flat_rows, up_weight, preferred_element_type=jnp.float32)
    hidden = ((up_value + 1.0) * gate_value * jax.nn.sigmoid(alpha_glu * gate_value)).astype(
        jnp.bfloat16
    )
    produced = jnp.dot(hidden, down_weight, preferred_element_type=jnp.float32).astype(jnp.bfloat16)
    return produced.reshape(received.shape)


def body(tokens, expert_ids, route_weights, w_gate, w_up, w_down):
    site_count = lax.axis_size("site")
    members = lax.axis_size("member")
    experts = EXP_SITE * site_count
    split_count = members // EXP_SITE
    tok_count = tokens.shape[0]
    top_count = expert_ids.shape[1]
    mean_rows = tok_count * top_count // experts
    most_rows = mean_rows + max(1, mean_rows // 8)
    gate_weight = w_gate[0]
    up_weight = w_up[0]
    down_weight = w_down[0]
    route_table = weight_table(expert_ids, route_weights, experts)
    needed = route_table > 0
    packed, clipped, group_ids = pack_rows(tokens, needed, most_rows)
    outgoing = jnp.repeat(packed, split_count, axis=0)
    produced = expert_apply(
        lax.all_to_all(outgoing, ("site", "member"), split_axis=0, concat_axis=0, tiled=True),
        gate_weight,
        up_weight,
        down_weight,
    )
    returned = lax.all_to_all(produced, ("site", "member"), split_axis=0, concat_axis=0, tiled=True)
    per_expert = jnp.sum(
        returned.astype(jnp.float32).reshape(experts, split_count, most_rows, -1), axis=1
    )
    picked = per_expert[group_ids, clipped]
    weighted = route_table.astype(jnp.float32)[:, :, None] * picked
    site_terms = jnp.sum(weighted.reshape(tok_count, site_count, EXP_SITE, -1), axis=2)
    rounded = lax.optimization_barrier(site_terms.astype(jnp.bfloat16))
    mixed_out = jnp.sum(rounded.astype(jnp.float32), axis=1)
    return mixed_out.astype(jnp.bfloat16)


def solution(mesh):
    placed = (
        P(("groups", "site", "member"), None),
        P(("groups", "site", "member"), None),
        P(("groups", "site", "member"), None),
        P(("site", "member"), None, None),
        P(("site", "member"), None, None),
        P(("site", "member"), None, None),
    )
    return jax.shard_map(
        body,
        mesh=mesh,
        in_specs=placed,
        out_specs=P(("groups", "site", "member"), None),
        check_vma=False,
    )
```

profile of v0, /device:TPU:11, one launch (start us, length us, event | category | flops | bytes accessed | tf_op | source)
XLA Modules:
  0.0 233.0 jit_solution(5532169070408501611)
XLA Ops:
  0.0 0.7 convert_element_type.50
  0.7 0.7 select_reduce_fusion
  1.4 0.1 copy.37
  1.5 0.1 reduce_window_sum.11
  1.6 0.1 copy.40
  1.7 0.7 multiply_reduce_fusion.1
  2.4 0.1 copy.42
  2.5 0.7 and_reduce_fusion
  3.2 0.1 copy.41
  3.4 0.1 reshape.103
  3.4 4.0 %broadcast_in_dim.39 = bf16[64,16,2880]{2,1,0:T(8,128)(2,1)} broadcast(bf16[64,2880]{1,0:T(8,128)(2,1)} %param.6), dimensions={0,2} | broadcast | bytes 6266880 | tf_op jit(solution)/shard_map/broadcast_in_dim | solution.py:24
  7.4 10.3 %scatter_custom_fusion = bf16[288,2880]{1,0:T(8,128)(2,1)S(1)} fusion(s32[1024]{0:T(1024)S(1)} %reshape.103, bf16[1024,2880]{1,0:T(8,128)(2,1)} %bitcast.35, bf16[]{:T(256)} %constant.9.clone.1), kind=kCustom, calls=%fused_computation.15 | custom fusion | bytes 1659392
  17.7 0.3 copy.43
  18.0 57.1 %all_to_all.10 = bf16[16,18,2880]{2,1,0:T(8,128)(2,1)S(1)} all-to-all(bf16[16,18,2880]{2,1,0:T(8,128)(2,1)S(1)} %copy.43), channel_id=1, replica_groups=mesh['groups'=2,'site'=4,'member'=4] {'site','member'}, dimensions={0} | all-to-all | bytes 3317760 | tf_op jit(solution)/shard_map/all_to_all | solution.py:58
  75.1 1.8 reshape.90
  76.9 0.0 copy-start
  76.9 0.0 slice-start
  76.9 0.0 slice-start.1
  76.9 0.0 slice-start.2
  76.9 10.0 %fusion.2 = f32[288,2880]{1,0:T(8,128)S(1)} fusion(bf16[288,2880]{1,0:T(8,128)(2,1)} %reshape.90, bf16[1,2880,2880]{2,1,0:T(8,128)(2,1)} %param.9), kind=kOutput, calls=%fused_computation.4 | convolution fusion | flops 4777574400 | bytes 21565440 | tf_op jit(solution)/shard_map/dot_general | solution.py:32
  87.0 0.0 copy-done
  87.0 0.0 slice-start.3
  87.0 0.0 slice-start.4
  87.0 9.7 %fusion.15 = bf16[288,2880]{1,0:T(8,128)(2,1)S(1)} fusion(f32[288,2880]{1,0:T(8,128)S(1)} %fusion.2, bf16[288,2880]{1,0:T(8,128)(2,1)S(1)} %copy-done, bf16[1,2880,2880]{2,1,0:T(8,128)(2,1)} %param.10), kind=kOutput, calls=%fused_computation.12 | convolution fusion | flops 4784209920 | bytes 23224320 | tf_op jit(solution)/shard_map/dot_general | solution.py:33
  96.7 0.0 slice-done
  96.7 0.0 slice-done.1
  96.8 0.0 slice-done.2
  96.8 0.0 slice-done.3
  96.8 0.0 slice-done.4
  96.8 5.6 %fusion.18 = bf16[288,2880]{1,0:T(8,128)(2,1)S(1)} fusion(bf16[288,2880]{1,0:T(8,128)(2,1)S(1)} %fusion.15, bf16[1,2880,2880]{2,1,0:T(8,128)(2,1)S(1)} %bitcast.38), kind=kOutput, calls=%fused_computation.13 | convolution fusion | flops 4778403840 | bytes 19906560 | tf_op jit(solution)/shard_map/dot_general | solution.py:37
  102.4 1.7 reshape.91
  104.1 5.9 %all-to-all-start.1 = ((bf16[16,18,2880]{2,1,0:T(8,128)(2,1)}), bf16[16,18,2880]{2,1,0:T(8,128)(2,1)}, u32[]{:S(2)}, u32[]{:S(2)}) async-start(bf16[16,18,2880]{2,1,0:T(8,128)(2,1)} %reshape.91), calls=%async_computation.1 | async-start | bytes 4521984 | tf_op jit(solution)/shard_map/all_to_all | solution.py:63
  110.0 0.1 copy.38
  110.1 0.1 reshape.97
  110.1 0.1 copy.39
  110.3 50.8 %all-to-all-done.1 = bf16[16,18,2880]{2,1,0:T(8,128)(2,1)} async-done(((bf16[16,18,2880]{2,1,0:T(8,128)(2,1)}), bf16[16,18,2880]{2,1,0:T(8,128)(2,1)}, u32[]{:S(2)}, u32[]{:S(2)}) %all-to-all-start.1) | async-done | bytes 1658912 | tf_op jit(solution)/shard_map/all_to_all | solution.py:63
  161.0 1.9 copy_convert_fusion
  162.9 22.7 %gather_fusion = f32[1024,2880]{1,0:T(8,128)} fusion(f32[16,18,2880]{2,0,1:T(8,128)S(1)} %copy_convert_fusion, s32[1024]{0:T(1024)S(1)} %reshape.97), kind=kCustom, calls=%fused_computation | custom fusion | bytes 23601152 | tf_op jit(solution)/shard_map/gather | solution.py:67
  185.6 14.2 %gather.6 = f32[64,4,4,2880]{3,2,1,0:T(4,128)} reshape(f32[1024,2880]{1,0:T(8,128)} %gather_fusion) | data formatting | bytes 23592960 | tf_op jit(solution)/shard_map/gather | solution.py:67
  199.8 30.4 %multiply_reduce_fusion = bf16[64,4,2880]{2,1,0:T(4,128)(2,1)S(1)} fusion(f32[64,4,4,2880]{3,2,1,0:T(4,128)} %gather.6, f32[64,4,4]{2,1,0:T(4,128)S(1)} %copy.39), kind=kLoop, calls=%fused_computation.8 | loop fusion | flops 5160960 | bytes 13275136 | tf_op jit(solution)/shard_map/reduce_sum | solution.py:69
  230.2 2.8 %reduce_sum.36 = bf16[64,2880]{1,0:T(8,128)(2,1)} reduce(bf16[64,4,2880]{2,1,0:T(4,128)(2,1)S(1)} %multiply_reduce_fusion, bf16[]{:T(256)} %constant.9.clone.1), dimensions={1}, to_apply=%region_4.5 | reduce | flops 552960 | bytes 1843202 | tf_op jit(solution)/shard_map/reduce_sum | solution.py:71
  (5 shorter events, 0.1 us)
Async XLA Ops:
  76.9 10.0 %copy-start = (bf16[288,2880]{1,0:T(8,128)(2,1)S(1)}, bf16[288,2880]{1,0:T(8,128)(2,1)}, u32[]{:S(2)}) copy-start(bf16[288,2880]{1,0:T(8,128)(2,1)} %reshape.90) | copy-start | bytes 4976644
  76.9 19.8 %slice-start = ((s8[16957440]{0:T(1024)(128)(4,1)}), s8[4194304]{0:T(1024)(128)(4,1)S(1)}, s32[]{:S(2)}) async-start(s8[16957440]{0:T(1024)(128)(4,1)} %bitcast.37), calls=%async_computation.2 | async-start | bytes 8388608
  76.9 19.8 %slice-start.1 = ((s8[16957440]{0:T(1024)(128)(4,1)}), s8[4194304]{0:T(1024)(128)(4,1)S(1)}, s32[]{:S(2)}) async-start(s8[16957440]{0:T(1024)(128)(4,1)} %bitcast.37), calls=%async_computation.3 | async-start | bytes 8388608
  76.9 19.8 %slice-start.2 = ((s8[16957440]{0:T(1024)(128)(4,1)}), s8[4194304]{0:T(1024)(128)(4,1)S(1)}, s32[]{:S(2)}) async-start(s8[16957440]{0:T(1024)(128)(4,1)} %bitcast.37), calls=%async_computation.4 | async-start | bytes 8388608
  87.0 9.8 %slice-start.3 = ((s8[16957440]{0:T(1024)(128)(4,1)}), s8[4194304]{0:T(1024)(128)(4,1)S(1)}, s32[]{:S(2)}) async-start(s8[16957440]{0:T(1024)(128)(4,1)} %bitcast.37), calls=%async_computation.5 | async-start | bytes 8388608
  87.0 9.8 %slice-start.4 = ((s8[16957440]{0:T(1024)(128)(4,1)}), s8[180224]{0:T(1024)(128)(4,1)S(1)}, s32[]{:S(2)}) async-start(s8[16957440]{0:T(1024)(128)(4,1)} %bitcast.37), calls=%async_computation.6 | async-start | bytes 360448
  104.1 57.0 %all-to-all-start.1 = ((bf16[16,18,2880]{2,1,0:T(8,128)(2,1)}), bf16[16,18,2880]{2,1,0:T(8,128)(2,1)}, u32[]{:S(2)}, u32[]{:S(2)}) async-start(bf16[16,18,2880]{2,1,0:T(8,128)(2,1)} %reshape.91), calls=%async_computation.1 | async-start | bytes 4521984 | tf_op jit(solution)/shard_map/all_to_all | solution.py:63
where the time goes:
time: 234 us; the launch traced here: 233 us
  blocking collectives  57.1 us (24%)
  local copies, waits for them, and re-layouts  55.7 us (24%)
  waiting for transfers between devices  50.8 us (22%)
  other arithmetic  38 us (16%)
  matrix products  25.3 us (11%)
  starting transfers between devices  5.9 us (3%)
    all_to_all x1, blocking collectives, body(): lax.all_to_all(outgoing, ('site', 'member'), split_axis=0, concat_axis=0,...  57.1 us
    all_to_all x1, waiting for transfers between devices, body(): lax.all_to_all(produced, ('site', 'member'), split_axis=0, concat_axis=0,...  50.8 us
    gather x2, local copies, waits for them, and re-layouts, body(): picked = per_expert[group_ids, clipped]  36.9 us
    reduce_sum x1, other arithmetic, body(): jnp.sum(weighted.reshape(tok_count, site_count, EXP_SITE, -1), axis=2)  30.4 us
    unnamed x16, local copies, waits for them, and re-layouts  10.6 us
    dot_general x1, matrix products, expert_apply(): jnp.dot(flat_rows, gate_weight, preferred_element_type=jnp.float32)  10 us
    dot_general x1, matrix products, expert_apply(): up_value = jnp.dot(flat_rows, up_weight, preferred_element_type=jnp.float32)  9.73 us
    all_to_all x1, starting transfers between devices, body(): lax.all_to_all(produced, ('site', 'member'), split_axis=0, concat_axis=0,...  5.9 us
  transfers between devices with their start and end apart: 1, of which 1 were waited for; matrix products, arithmetic and copies ran while one was open for 0% of the time, Pallas kernels for 0%

commit v1 on v0

v1 whole, which is shorter than its diff:
```python
import functools

import jax
import jax.numpy as jnp
from jax import lax
from jax.experimental import pallas as pl
from jax.experimental.pallas import tpu as pltpu
from jax.sharding import PartitionSpec as P

EXP_SITE = 4
LANE = 128
SUB = 8
TILE = 512

alpha_glu = 1.702


class Fold:
    def __init__(self, rows, width):
        self.rows = rows
        self.width = width
        self.padded = -(-width // LANE) * LANE
        self.groups = rows // SUB
        self.rest = rows % SUB
        if self.rest and SUB % self.rest:
            self.groups, self.rest = self.groups + 1, 0
        self.pieces = SUB // self.rest if self.rest else 0
        tiles = self.padded // LANE
        self.piece = -(-tiles // self.pieces) * LANE if self.rest else 0
        self.tail_at = self.groups * self.padded
        self.total = self.tail_at + self.piece
        self.slots = self.groups * SUB + self.rest

    def spans(self):
        for p in range(self.pieces):
            lo = p * self.piece
            hi = min(self.width, lo + self.piece)
            if hi > lo:
                yield p, lo, hi


def slot_masks(route, fold, chunks):
    half = route.shape[0] // 2
    tokens = route.shape[1]
    shape = (chunks * SUB, tokens)
    row = lax.broadcasted_iota(jnp.int32, shape, 0)
    group = (row // SUB).astype(jnp.float32)
    sub = row % SUB
    need = jnp.zeros(shape, jnp.float32)
    weight = jnp.zeros(shape, jnp.float32)
    for k in range(half):
        hit = route[k : k + 1, :] == group
        need = jnp.where(hit, 1.0, need)
        weight = jnp.where(hit, route[half + k : half + k + 1, :], weight)
    before = (
        lax.broadcasted_iota(jnp.int32, (tokens, tokens), 0)
        < lax.broadcasted_iota(jnp.int32, (tokens, tokens), 1)
    ).astype(jnp.bfloat16)
    position = jnp.dot(need.astype(jnp.bfloat16), before, preferred_element_type=jnp.float32)
    position = jnp.where(need > 0, position, -1.0)
    subf = sub.astype(jnp.float32)
    mains = [position == subf + float(SUB * q) for q in range(fold.groups)]
    tails = []
    for p in range(fold.pieces):
        slot = (sub // fold.pieces).astype(jnp.float32) + float(SUB * fold.groups)
        tails.append((position == slot) & (sub % fold.pieces == p))
    return mains, tails, weight


def pack_kernel(fold, chunks, route_ref, tokens_ref, out_ref):
    mains, tails, _ = slot_masks(route_ref[...], fold, chunks)
    for q, mask in enumerate(mains):
        pick = jnp.where(mask, 1.0, 0.0).astype(jnp.bfloat16)
        rows = jnp.dot(pick, tokens_ref[...], preferred_element_type=jnp.float32)
        lo = q * fold.padded
        out_ref[:, lo : lo + fold.width] = rows.astype(jnp.bfloat16)
    if tails:
        total = None
        for p, lo, hi in fold.spans():
            pick = jnp.where(tails[p], 1.0, 0.0).astype(jnp.bfloat16)
            piece = jnp.dot(pick, tokens_ref[:, lo:hi], preferred_element_type=jnp.float32)
            if hi - lo < fold.piece:
                blank = jnp.zeros((piece.shape[0], fold.piece - (hi - lo)), jnp.float32)
                piece = jnp.concatenate([piece, blank], axis=1)
            total = piece if total is None else total + piece
        out_ref[:, fold.tail_at :] = total.astype(jnp.bfloat16)


def weighted_sum(fold, chunks, route, returned_ref):
    mains, tails, weight = slot_masks(route, fold, chunks)
    contract = (((0,), (0,)), ((), ()))
    total = None
    for q, mask in enumerate(mains):
        scale = jnp.where(mask, weight, 0.0).astype(jnp.bfloat16)
        lo = q * fold.padded
        term = lax.dot_general(
            scale,
            returned_ref[:, lo : lo + fold.width],
            contract,
            preferred_element_type=jnp.float32,
        )
        total = term if total is None else total + term
    if tails:
        pieces = []
        for p, lo, hi in fold.spans():
            scale = jnp.where(tails[p], weight, 0.0).astype(jnp.bfloat16)
            pieces.append(
                lax.dot_general(
                    scale,
                    returned_ref[:, fold.tail_at : fold.tail_at + (hi - lo)],
                    contract,
                    preferred_element_type=jnp.float32,
                )
            )
        term = jnp.concatenate(pieces, axis=1)
        total = term if total is None else total + term
    return total


def held_kernel(fold, chunks, route_ref, returned_ref, out_ref):
    out_ref[...] = weighted_sum(fold, chunks, route_ref[...], returned_ref).astype(jnp.bfloat16)


def final_kernel(fold, chunks, route_ref, returned_ref, other_ref, out_ref):
    total = weighted_sum(fold, chunks, route_ref[...], returned_ref)
    out_ref[...] = (total + other_ref[...].astype(jnp.float32)).astype(jnp.bfloat16)


def tail_pick(fold, sources, p):
    shape = (sources * fold.rest, sources * SUB)
    row = lax.broadcasted_iota(jnp.int32, shape, 0)
    col = lax.broadcasted_iota(jnp.int32, shape, 1)
    want = (row // fold.rest) * SUB + (row % fold.rest) * fold.pieces + p
    return jnp.where(col == want, 1.0, 0.0).astype(jnp.bfloat16)


def expert_kernel(
    fold, sources, up_steps, own_ref, far_ref, gate_ref, up_ref, down_ref,
    own_out, far_out, x_ref, h_ref, o_ref,
):
    step = pl.program_id(0)
    width = fold.width
    ff = h_ref.shape[1]
    part = sources * fold.slots
    block = sources * SUB

    @pl.when(step == 0)
    def _():
        for base, src in ((0, own_ref), (part, far_ref)):
            for q in range(fold.groups):
                lo = q * fold.padded
                x_ref[base + q * block : base + (q + 1) * block, :] = src[:, lo : lo + width]
            at = base + fold.groups * block
            for p, lo, hi in fold.spans():
                rows = jnp.dot(
                    tail_pick(fold, sources, p),
                    src[:, fold.tail_at : fold.tail_at + (hi - lo)],
                    preferred_element_type=jnp.float32,
                )
                x_ref[at : at + sources * fold.rest, lo:hi] = rows.astype(jnp.bfloat16)

    @pl.when(step < up_steps)
    def _():
        gate = jnp.dot(x_ref[...], gate_ref[0], preferred_element_type=jnp.float32)
        up = jnp.dot(x_ref[...], up_ref[0], preferred_element_type=jnp.float32)
        hidden = ((up + 1.0) * gate * jax.nn.sigmoid(alpha_glu * gate)).astype(jnp.bfloat16)
        tile = hidden.shape[1]
        for t in range(up_steps):
            lo = t * tile
            hi = min(ff, lo + tile)

            @pl.when(step == t)
            def _():
                h_ref[:, lo:hi] = hidden[:, : hi - lo]

    @pl.when(step >= up_steps)
    def _():
        made = jnp.dot(h_ref[...], down_ref[0], preferred_element_type=jnp.float32)
        made = made.astype(jnp.bfloat16)
        tile = made.shape[1]
        down_steps = -(-width // tile)
        for t in range(down_steps):
            lo = t * tile
            hi = min(width, lo + tile)

            @pl.when(step == up_steps + t)
            def _():
                o_ref[:, lo:hi] = made[:, : hi - lo]

    @pl.when(step == pl.num_programs(0) - 1)
    def _():
        for base, dst in ((0, own_out), (part, far_out)):
            for q in range(fold.groups):
                lo = q * fold.padded
                dst[:, lo : lo + width] = o_ref[base + q * block : base + (q + 1) * block, :]
            at = base + fold.groups * block
            total = None
            for p, lo, hi in fold.spans():
                rows = lax.dot_general(
                    tail_pick(fold, sources, p),
                    o_ref[at : at + sources * fold.rest, lo:hi],
                    (((0,), (0,)), ((), ())),
                    preferred_element_type=jnp.float32,
                )
                if hi - lo < fold.piece:
                    blank = jnp.zeros((rows.shape[0], fold.piece - (hi - lo)), jnp.float32)
                    rows = jnp.concatenate([rows, blank], axis=1)
                total = rows if total is None else total + rows
            if total is not None:
                dst[:, fold.tail_at :] = total.astype(jnp.bfloat16)


def whole_block(shape):
    return pl.BlockSpec(shape, lambda *_: (0,) * len(shape), pipeline_mode=pl.Buffered(1))


def run_experts(fold, sources, own, far, w_gate, w_up, w_down):
    width, ff = w_gate.shape[1], w_gate.shape[2]
    up_tile = min(TILE, ff)
    down_tile = min(TILE, width)
    up_steps = -(-ff // up_tile)
    down_steps = -(-width // down_tile)
    rows = 2 * sources * fold.slots
    up_spec = pl.BlockSpec((1, width, up_tile), lambda i: (0, 0, jnp.minimum(i, up_steps - 1)))
    down_spec = pl.BlockSpec((1, ff, down_tile), lambda i: (0, 0, jnp.maximum(i - up_steps, 0)))
    return pl.pallas_call(
        functools.partial(expert_kernel, fold, sources, up_steps),
        out_shape=(jax.ShapeDtypeStruct(own.shape, own.dtype),) * 2,
        grid=(up_steps + down_steps,),
        in_specs=[whole_block(own.shape), whole_block(far.shape), up_spec, up_spec, down_spec],
        out_specs=(whole_block(own.shape),) * 2,
        scratch_shapes=[
            pltpu.VMEM((rows, width), jnp.bfloat16),
            pltpu.VMEM((rows, ff), jnp.bfloat16),
            pltpu.VMEM((rows, width), jnp.bfloat16),
        ],
        name="experts",
        cost_estimate=pl.CostEstimate(
            flops=6 * rows * width * ff,
            bytes_accessed=6 * width * ff + 8 * own.size,
            transcendentals=rows * ff,
        ),
    )(own, far, w_gate, w_up, w_down)


def body(tokens, expert_ids, route_weights, w_gate, w_up, w_down):
    site_count = lax.axis_size("site")
    members = lax.axis_size("member")
    experts = EXP_SITE * site_count
    split = members // EXP_SITE
    tok_count, width = tokens.shape
    top_count = expert_ids.shape[1]
    mean_rows = tok_count * top_count // experts
    most_rows = mean_rows + max(1, mean_rows // 8)
    half = site_count // 2
    chunks = experts // 2
    sources = half * members
    fold = Fold(most_rows, width)

    swap = [(s, (s + half) % site_count) for s in range(site_count)]
    halves = [list(range(h * sources, (h + 1) * sources)) for h in range(2)]
    first = (lax.axis_index("site") // half * chunks).astype(jnp.float32)

    def exchange(value):
        return lax.all_to_all(
            value, ("site", "member"), split_axis=0, concat_axis=0, tiled=True,
            axis_index_groups=halves,
        )

    def local(route):
        return jnp.concatenate([route[:top_count] - first, route[top_count:]], axis=0)

    def pack(route, rows):
        packed = pl.pallas_call(
            functools.partial(pack_kernel, fold, chunks),
            out_shape=jax.ShapeDtypeStruct((chunks * SUB, fold.total), rows.dtype),
            name="pack",
        )(route, rows)
        if split > 1:
            packed = jnp.repeat(packed.reshape(chunks, SUB, -1), split, axis=0)
            packed = packed.reshape(sources * SUB, -1)
        return packed

    route = jnp.concatenate(
        [expert_ids.T.astype(jnp.float32), route_weights.T.astype(jnp.float32)], axis=0
    )
    far_tokens = lax.ppermute(tokens, "site", swap)
    far_route = local(lax.ppermute(route, "site", swap))
    route = local(route)

    own_in = exchange(pack(route, tokens))
    far_in = exchange(pack(far_route, far_tokens))
    own_made, far_made = run_experts(fold, sources, own_in, far_in, w_gate, w_up, w_down)

    def spread(value):
        if split == 1:
            return value
        value = value.reshape(chunks, split, SUB, -1)
        return jnp.sum(value.astype(jnp.float32), axis=1).astype(value.dtype).reshape(chunks * SUB, -1)

    far_back = spread(exchange(far_made))
    far_sum = pl.pallas_call(
        functools.partial(held_kernel, fold, chunks),
        out_shape=jax.ShapeDtypeStruct(tokens.shape, tokens.dtype),
        name="held",
    )(far_route, far_back)
    own_made, far_sum = lax.optimization_barrier((own_made, far_sum))
    other = lax.ppermute(far_sum, "site", [(b, a) for a, b in swap])
    own_back = spread(exchange(own_made))
    return pl.pallas_call(
        functools.partial(final_kernel, fold, chunks),
        out_shape=jax.ShapeDtypeStruct(tokens.shape, tokens.dtype),
        name="final",
    )(route, own_back, other)


def solution(mesh):
    placed = (
        P(("groups", "site", "member"), None),
        P(("groups", "site", "member"), None),
        P(("groups", "site", "member"), None),
        P(("site", "member"), None, None),
        P(("site", "member"), None, None),
        P(("site", "member"), None, None),
    )
    return jax.shard_map(
        body,
        mesh=mesh,
        in_specs=placed,
        out_specs=P(("groups", "site", "member"), None),
        check_vma=False,
    )
```

time: 234 us -> 130 us (0.56)
  local copies, waits for them, and re-layouts: 55.7 us -> 1.79 us
  Pallas kernels: 0 us -> 38.9 us
  other arithmetic: 38 us -> 3.25 us
  matrix products: 25.3 us -> 0 us
  blocking collectives: 57.1 us -> 33.1 us
  waiting for transfers between devices: 50.8 us -> 36.3 us
  starting transfers between devices: 5.9 us -> 14 us
    all_to_all x1 -> x2, waiting for transfers between devices: 50.8 us -> 0.01 us  [exchange(): lax.all_to_all(value, ('site', 'member'), split_axis=0, concat_axis=0, ti...]
    pallas_call x0 -> x5, Pallas kernels: none -> 38.9 us  [the longest x1 28.8 us: run_experts(): pl.pallas_call(functools.partial(expert_kernel, fold, sources, up_steps),...]
    gather x2 -> x0, local copies, waits for them, and re-layouts: 36.9 us -> none  [body(): picked = per_expert[group_ids, clipped]]
    ppermute x0 -> x3, waiting for transfers between devices: none -> 36.3 us  [the longest x1 18.2 us: body(): far_route = local(lax.ppermute(route, 'site', swap))]
    reduce_sum x3 -> x0, other arithmetic: 33.9 us -> none  [the longest x1 30.4 us: body(): jnp.sum(weighted.reshape(tok_count, site_count, EXP_SITE, -1), axis=2)]
    dot_general x3 -> x0, matrix products: 25.3 us -> none  [the longest x1 10 us: expert_apply(): jnp.dot(flat_rows, gate_weight, preferred_element_type=jnp.float32)]
    all_to_all x1 -> x2, blocking collectives: 57.1 us -> 33.1 us  [exchange(): lax.all_to_all(value, ('site', 'member'), split_axis=0, concat_axis=0, ti...]
    unnamed x16 -> x8, local copies, waits for them, and re-layouts: 10.6 us -> 1.79 us
  transfers between devices with their start and end apart: 1 -> 5, of which waited for: 1 -> 2; matrix products, arithmetic and copies ran while one was open for 0% -> 0% of each run, Pallas kernels for 0% -> 2%
where the time goes in v1:
time: 130 us; the launch traced here: 127 us
  Pallas kernels  38.9 us (30%)
  waiting for transfers between devices  36.3 us (28%)
  blocking collectives  33.1 us (25%)
  starting transfers between devices  14 us (11%)
  other arithmetic  3.25 us (2%)
  local copies, waits for them, and re-layouts  1.79 us (1%)
    all_to_all x2, blocking collectives, exchange(): lax.all_to_all(value, ('site', 'member'), split_axis=0, concat_axis=0, ti...  33.1 us
    pallas_call x1, Pallas kernels, run_experts(): pl.pallas_call(functools.partial(expert_kernel, fold, sources, up_steps),...  28.8 us
    ppermute x1, waiting for transfers between devices, body(): far_route = local(lax.ppermute(route, 'site', swap))  18.2 us
    ppermute x1, waiting for transfers between devices, body(): other = lax.ppermute(far_sum, 'site', [(b, a) for a, b in swap])  18.1 us
    all_to_all x2, starting transfers between devices, exchange(): lax.all_to_all(value, ('site', 'member'), split_axis=0, concat_axis=0, ti...  10.3 us
    pallas_call x2, Pallas kernels, pack(): pl.pallas_call(functools.partial(pack_kernel, fold, chunks), out_shape=ja...  4.96 us
    pallas_call x1, Pallas kernels, body(): pl.pallas_call(functools.partial(final_kernel, fold, chunks), out_shape=j...  2.62 us
  transfers between devices with their start and end apart: 5, of which 2 were waited for; matrix products, arithmetic and copies ran while one was open for 0% of the time, Pallas kernels for 2%

profile of v1, /device:TPU:11, one launch (start us, length us, event | category | flops | bytes accessed | tf_op | source)
XLA Modules:
  0.0 127.5 jit_solution(9398823630637392581)
XLA Ops:
  0.0 0.7 convert_bitcast_fusion
  0.7 0.7 convert_bitcast_fusion.1
  1.4 0.7 broadcast_subtract_fusion
  2.1 0.6 pad_maximum_fusion
  2.7 2.5 %pack.2 = bf16[64,6656]{1,0:T(8,128)(2,1)} custom-call(f32[8,64]{1,0:T(8,128)} %get-tuple-element.16.route_ref, bf16[64,2880]{1,0:T(8,128)(2,1)} %tokens_ref.1), custom_call_target="tpu_custom_call" | custom-call | tf_op jit(solution)/shard_map/pack/pallas_call | solution.py:274
  5.1 4.5 %all-to-all-start = ((bf16[8,8,6656]{2,1,0:T(8,128)(2,1)}), bf16[8,8,6656]{2,1,0:T(8,128)(2,1)S(1)}, u32[]{:S(2)}, u32[]{:S(2)}) async-start(bf16[8,8,6656]{2,1,0:T(8,128)(2,1)} %bitcast.14), calls=%async_computation | async-start | bytes 1703936 | tf_op jit(solution)/shard_map/all_to_all | solution.py:265
  9.6 2.3 %collective-permute-start.1 = (bf16[64,2880]{1,0:T(8,128)(2,1)}, bf16[64,2880]{1,0:T(8,128)(2,1)S(1)}, u32[]{:S(2)}, u32[]{:S(2)}) collective-permute-start(bf16[64,2880]{1,0:T(8,128)(2,1)} %tokens_ref.1), channel_id=1, source_target_pairs={{0,8},{4,12},{8,0},{12,4},{1,9},{5,13},{9,1},{13,5},{2,10},{6,14},... | collective-permute-start | bytes 1105928 | tf_op jit(solution)/shard_map/ppermute | solution.py:287
  11.9 0.1 collective-permute-start
  12.0 18.2 %collective-permute-done = f32[8,64]{1,0:T(8,128)S(1)} collective-permute-done((f32[8,64]{1,0:T(8,128)S(1)}, f32[8,64]{1,0:T(8,128)S(1)}, u32[]{:S(2)}, u32[]{:S(2)}) %collective-permute-start) | collective-permute-done | bytes 2080 | tf_op jit(solution)/shard_map/ppermute | solution.py:288
  30.2 0.6 pad_maximum_fusion.2.route_ref
  30.8 0.0 collective-permute-done.1.tokens_ref
  30.8 0.0 copy-start.2
  30.8 0.7 copy-done.2
  31.5 2.5 %pack.3 = bf16[64,6656]{1,0:T(8,128)(2,1)} custom-call(f32[8,64]{1,0:T(8,128)} %pad_maximum_fusion.2.route_ref, bf16[64,2880]{1,0:T(8,128)(2,1)} %copy-done.2), custom_call_target="tpu_custom_call" | custom-call | tf_op jit(solution)/shard_map/pack/pallas_call | solution.py:274
  34.0 0.0 all-to-all-done
  34.0 0.0 copy-start.1
  34.0 15.7 %all_to_all.44 = bf16[8,8,6656]{2,1,0:T(8,128)(2,1)} all-to-all(bf16[8,8,6656]{2,1,0:T(8,128)(2,1)} %bitcast.16), channel_id=1, replica_groups={{0,1,2,3,4,5,6,7},{8,9,10,11,12,13,14,15},{16,17,18,19,20,21,22,23},{24..., dimensions={0} | all-to-all | bytes 1703936 | tf_op jit(solution)/shard_map/all_to_all | solution.py:265
  49.7 0.0 copy-done.1
  49.7 28.8 %experts.1 = (bf16[64,6656]{1,0:T(8,128)(2,1)}, bf16[64,6656]{1,0:T(8,128)(2,1)}) custom-call(bf16[64,6656]{1,0:T(8,128)(2,1)} %bitcast.18, bf16[64,6656]{1,0:T(8,128)(2,1)} %bitcast.20, bf16[1,2880,2880]{2,1,0:T(8,128)(2,1)} %gate_ref.1, bf16[1,2880,2880]{2,1,0:T(8,128)(2,1)} %up_ref.1, bf16[1,2880,2880]{2,1,0:T(8,128)(2,1)} %down_ref.1), custom_call_target="tpu_custom_call" | custom-call | flops 14332723200 | bytes 53174272 | tf_op jit(solution)/shard_map/experts/pallas_call | solution.py:226
  78.5 17.4 %all_to_all.45 = bf16[8,8,6656]{2,1,0:T(8,128)(2,1)} all-to-all(bf16[8,8,6656]{2,1,0:T(8,128)(2,1)} %bitcast.21), channel_id=1, replica_groups={{0,1,2,3,4,5,6,7},{8,9,10,11,12,13,14,15},{16,17,18,19,20,21,22,23},{24..., dimensions={0} | all-to-all | bytes 1703936 | tf_op jit(solution)/shard_map/all_to_all | solution.py:265
  95.9 2.5 %held.1 = bf16[64,2880]{1,0:T(8,128)(2,1)} custom-call(f32[8,64]{1,0:T(8,128)} %pad_maximum_fusion.2.route_ref, bf16[64,6656]{1,0:T(8,128)(2,1)} %bitcast.17), custom_call_target="tpu_custom_call" | custom-call | tf_op jit(solution)/shard_map/held/pallas_call | solution.py:302
  98.5 5.8 %all-to-all-start.3 = ((bf16[8,8,6656]{2,1,0:T(8,128)(2,1)}), bf16[8,8,6656]{2,1,0:T(8,128)(2,1)S(1)}, u32[]{:S(2)}, u32[]{:S(2)}) async-start(bf16[8,8,6656]{2,1,0:T(8,128)(2,1)} %bitcast.19), calls=%async_computation.3 | async-start | bytes 1703936 | tf_op jit(solution)/shard_map/all_to_all | solution.py:265
  104.3 1.4 %collective-permute-start.2 = (bf16[64,2880]{1,0:T(8,128)(2,1)}, bf16[64,2880]{1,0:T(8,128)(2,1)S(1)}, u32[]{:S(2)}, u32[]{:S(2)}) collective-permute-start(bf16[64,2880]{1,0:T(8,128)(2,1)} %held.1), channel_id=1, source_target_pairs={{8,0},{12,4},{0,8},{4,12},{9,1},{13,5},{1,9},{5,13},{10,2},{14,6},... | collective-permute-start | bytes 1105928 | tf_op jit(solution)/shard_map/ppermute | solution.py:308
  105.7 18.1 %collective-permute-done.2.other_ref = bf16[64,2880]{1,0:T(8,128)(2,1)S(1)} collective-permute-done((bf16[64,2880]{1,0:T(8,128)(2,1)}, bf16[64,2880]{1,0:T(8,128)(2,1)S(1)}, u32[]{:S(2)}, u32[]{:S(2)}) %collective-permute-start.2) | collective-permute-done | bytes 368672 | tf_op jit(solution)/shard_map/ppermute | solution.py:308
  123.8 0.0 copy-start.3
  123.8 0.0 all-to-all-done.3
  123.8 0.0 copy-start
  123.8 0.7 copy-done.3
  124.5 0.3 copy-done
  124.8 2.6 %final.1 = bf16[64,2880]{1,0:T(8,128)(2,1)} custom-call(f32[8,64]{1,0:T(8,128)} %get-tuple-element.16.route_ref, bf16[64,6656]{1,0:T(8,128)(2,1)} %bitcast.15, bf16[64,2880]{1,0:T(8,128)(2,1)} %copy-done.3), custom_call_target="tpu_custom_call" | custom-call | tf_op jit(solution)/shard_map/final/pallas_call | solution.py:310
  (1 shorter events, 0.0 us)
Async XLA Ops:
  5.1 28.8 %all-to-all-start = ((bf16[8,8,6656]{2,1,0:T(8,128)(2,1)}), bf16[8,8,6656]{2,1,0:T(8,128)(2,1)S(1)}, u32[]{:S(2)}, u32[]{:S(2)}) async-start(bf16[8,8,6656]{2,1,0:T(8,128)(2,1)} %bitcast.14), calls=%async_computation | async-start | bytes 1703936 | tf_op jit(solution)/shard_map/all_to_all | solution.py:265
  9.6 21.1 %collective-permute-start.1 = (bf16[64,2880]{1,0:T(8,128)(2,1)}, bf16[64,2880]{1,0:T(8,128)(2,1)S(1)}, u32[]{:S(2)}, u32[]{:S(2)}) collective-permute-start(bf16[64,2880]{1,0:T(8,128)(2,1)} %tokens_ref.1), channel_id=1, source_target_pairs={{0,8},{4,12},{8,0},{12,4},{1,9},{5,13},{9,1},{13,5},{2,10},{6,14},... | collective-permute-start | bytes 1105928 | tf_op jit(solution)/shard_map/ppermute | solution.py:287
  11.9 18.2 %collective-permute-start = (f32[8,64]{1,0:T(8,128)S(1)}, f32[8,64]{1,0:T(8,128)S(1)}, u32[]{:S(2)}, u32[]{:S(2)}) collective-permute-start(f32[8,64]{1,0:T(8,128)S(1)} %get-tuple-element.15), channel_id=1, source_target_pairs={{0,8},{4,12},{8,0},{12,4},{1,9},{5,13},{9,1},{13,5},{2,10},{6,14},... | collective-permute-start | bytes 6152 | tf_op jit(solution)/shard_map/ppermute | solution.py:288
  30.8 0.7 copy-start.2
  34.0 15.7 %copy-start.1 = (bf16[8,8,6656]{2,1,0:T(8,128)(2,1)}, bf16[8,8,6656]{2,1,0:T(8,128)(2,1)S(1)}, u32[]{:S(2)}) copy-start(bf16[8,8,6656]{2,1,0:T(8,128)(2,1)S(1)} %all-to-all-done) | copy-start | bytes 2555908
  98.5 25.3 %all-to-all-start.3 = ((bf16[8,8,6656]{2,1,0:T(8,128)(2,1)}), bf16[8,8,6656]{2,1,0:T(8,128)(2,1)S(1)}, u32[]{:S(2)}, u32[]{:S(2)}) async-start(bf16[8,8,6656]{2,1,0:T(8,128)(2,1)} %bitcast.19), calls=%async_computation.3 | async-start | bytes 1703936 | tf_op jit(solution)/shard_map/all_to_all | solution.py:265
  104.3 19.5 %collective-permute-start.2 = (bf16[64,2880]{1,0:T(8,128)(2,1)}, bf16[64,2880]{1,0:T(8,128)(2,1)S(1)}, u32[]{:S(2)}, u32[]{:S(2)}) collective-permute-start(bf16[64,2880]{1,0:T(8,128)(2,1)} %held.1), channel_id=1, source_target_pairs={{8,0},{12,4},{0,8},{4,12},{9,1},{13,5},{1,9},{5,13},{10,2},{14,6},... | collective-permute-start | bytes 1105928 | tf_op jit(solution)/shard_map/ppermute | solution.py:308
  123.8 0.8 copy-start.3
  123.8 1.0 copy-start

commit v2 on v0

v2 whole, which is shorter than its diff:
```python
import functools

import jax
import jax.numpy as jnp
from jax import lax
from jax.experimental import pallas as pl
from jax.experimental.pallas import tpu as pltpu
from jax.sharding import PartitionSpec as P

EXP_SITE = 4
LANE = 128
SUB = 8
TILE = 512
DEPTH = 3
MOST_PERMUTES = 8
SMALL = 12 << 20
MIDDLE = 44 << 20
LARGE = 60 * 1024 * 1024

alpha_glu = 1.702


class Fold:
    def __init__(self, rows, width):
        self.rows = rows
        self.width = width
        self.padded = -(-width // LANE) * LANE
        self.groups = rows // SUB
        self.rest = rows % SUB
        if self.rest and SUB % self.rest:
            self.groups, self.rest = self.groups + 1, 0
        self.pieces = SUB // self.rest if self.rest else 0
        tiles = self.padded // LANE
        self.piece = -(-tiles // self.pieces) * LANE if self.rest else 0
        self.tail_at = self.groups * self.padded
        self.total = self.tail_at + self.piece
        self.slots = self.groups * SUB + self.rest

    def spans(self):
        for p in range(self.pieces):
            lo = p * self.piece
            hi = min(self.width, lo + self.piece)
            if hi > lo:
                yield p, lo, hi


class Plan:
    def __init__(self, half, members, chunks, fold, ff):
        self.half = half
        self.members = members
        self.chunks = chunks
        self.sources = half * members
        self.split = self.sources // chunks
        self.pairwise = self.sources <= MOST_PERMUTES and self.sources & (self.sources - 1) == 0
        self.fold = fold
        self.ff = ff
        self.parts = self.sources if self.pairwise else 1
        self.part_rows = self.sources * SUB // self.parts

    def expert_of(self, chunk):
        site = lax.axis_index("site")
        if self.pairwise:
            me = site % self.half * self.members + lax.axis_index("member")
            chunk = jnp.bitwise_xor(chunk, me)
        return site // self.half * self.chunks + chunk // self.split

    def gather(self, refs, stage_ref):
        for k, ref in enumerate(refs):
            stage_ref[k * self.part_rows : (k + 1) * self.part_rows, :] = ref[...]

    def scatter(self, stage_ref, refs):
        for k, ref in enumerate(refs):
            ref[...] = stage_ref[k * self.part_rows : (k + 1) * self.part_rows, :]

    @property
    def stage(self):
        return pltpu.VMEM((self.sources * SUB, self.fold.total), jnp.bfloat16)

    @property
    def part_shape(self):
        return jax.ShapeDtypeStruct((self.part_rows, self.fold.total), jnp.bfloat16)


def slot_masks(route, plan):
    fold = plan.fold
    top = route.shape[0] // 2
    tokens = route.shape[1]
    shape = (plan.sources * SUB, tokens)
    row = lax.broadcasted_iota(jnp.int32, shape, 0)
    group = plan.expert_of(row // SUB).astype(jnp.float32)
    sub = row % SUB
    need = jnp.zeros(shape, jnp.float32)
    weight = jnp.zeros(shape, jnp.float32)
    for k in range(top):
        hit = route[k : k + 1, :] == group
        need = jnp.where(hit, 1.0, need)
        weight = jnp.where(hit, route[top + k : top + k + 1, :], weight)
    before = (
        lax.broadcasted_iota(jnp.int32, (tokens, tokens), 0)
        < lax.broadcasted_iota(jnp.int32, (tokens, tokens), 1)
    ).astype(jnp.bfloat16)
    position = jnp.dot(need.astype(jnp.bfloat16), before, preferred_element_type=jnp.float32)
    position = jnp.where(need > 0, position, -1.0)
    subf = sub.astype(jnp.float32)
    mains = [position == subf + float(SUB * q) for q in range(fold.groups)]
    tails = []
    for p in range(fold.pieces):
        slot = (sub // fold.pieces).astype(jnp.float32) + float(SUB * fold.groups)
        tails.append((position == slot) & (sub % fold.pieces == p))
    return mains, tails, weight


def pack_rows(route, plan, tokens_ref, out_ref):
    fold = plan.fold
    mains, tails, _ = slot_masks(route, plan)
    for q, mask in enumerate(mains):
        pick = jnp.where(mask, 1.0, 0.0).astype(jnp.bfloat16)
        rows = jnp.dot(pick, tokens_ref[...], preferred_element_type=jnp.float32)
        lo = q * fold.padded
        out_ref[:, lo : lo + fold.width] = rows.astype(jnp.bfloat16)
    if tails:
        total = None
        for p, lo, hi in fold.spans():
            pick = jnp.where(tails[p], 1.0, 0.0).astype(jnp.bfloat16)
            piece = jnp.dot(pick, tokens_ref[:, lo:hi], preferred_element_type=jnp.float32)
            if hi - lo < fold.piece:
                blank = jnp.zeros((piece.shape[0], fold.piece - (hi - lo)), jnp.float32)
                piece = jnp.concatenate([piece, blank], axis=1)
            total = piece if total is None else total + piece
        out_ref[:, fold.tail_at :] = total.astype(jnp.bfloat16)


def own_pack_kernel(plan, ids_ref, weights_ref, tokens_ref, *refs):
    out_refs, route_ref, stage_ref = refs[:-2], refs[-2], refs[-1]
    top = ids_ref.shape[0]
    route_ref[0:top, :] = ids_ref[...].astype(jnp.float32)
    route_ref[top:, :] = weights_ref[...].astype(jnp.float32)
    pack_rows(route_ref[...], plan, tokens_ref, stage_ref)
    plan.scatter(stage_ref, out_refs)


def far_pack_kernel(plan, route_ref, tokens_ref, *refs):
    out_refs, stage_ref = refs[:-1], refs[-1]
    pack_rows(route_ref[...], plan, tokens_ref, stage_ref)
    plan.scatter(stage_ref, out_refs)


def weighted_sum(plan, route, returned_ref):
    fold = plan.fold
    mains, tails, weight = slot_masks(route, plan)
    contract = (((0,), (0,)), ((), ()))
    total = None
    for q, mask in enumerate(mains):
        scale = jnp.where(mask, weight, 0.0).astype(jnp.bfloat16)
        lo = q * fold.padded
        term = lax.dot_general(
            scale,
            returned_ref[:, lo : lo + fold.width],
            contract,
            preferred_element_type=jnp.float32,
        )
        total = term if total is None else total + term
    if tails:
        pieces = []
        for p, lo, hi in fold.spans():
            scale = jnp.where(tails[p], weight, 0.0).astype(jnp.bfloat16)
            pieces.append(
                lax.dot_general(
                    scale,
                    returned_ref[:, fold.tail_at : fold.tail_at + (hi - lo)],
                    contract,
                    preferred_element_type=jnp.float32,
                )
            )
        term = jnp.concatenate(pieces, axis=1)
        total = term if total is None else total + term
    return total


def held_kernel(plan, route_ref, *refs):
    in_refs, out_ref, stage_ref = refs[:-2], refs[-2], refs[-1]
    plan.gather(in_refs, stage_ref)
    out_ref[...] = weighted_sum(plan, route_ref[...], stage_ref).astype(jnp.bfloat16)


def final_kernel(plan, route_ref, other_ref, *refs):
    in_refs, out_ref, stage_ref = refs[:-2], refs[-2], refs[-1]
    plan.gather(in_refs, stage_ref)
    total = weighted_sum(plan, route_ref[...], stage_ref)
    out_ref[...] = (total + other_ref[...].astype(jnp.float32)).astype(jnp.bfloat16)


def tail_pick(fold, sources, p):
    shape = (sources * fold.rest, sources * SUB)
    row = lax.broadcasted_iota(jnp.int32, shape, 0)
    col = lax.broadcasted_iota(jnp.int32, shape, 1)
    want = (row // fold.rest) * SUB + (row % fold.rest) * fold.pieces + p
    return jnp.where(col == want, 1.0, 0.0).astype(jnp.bfloat16)


def column_tiles(count):
    tiles, at = [], 0
    while count - at >= LANE:
        size = min(TILE // 2 if at < TILE else TILE, (count - at) // LANE * LANE)
        if count - at - size < LANE:
            size = count - at
        tiles.append((at, size))
        at += size
    if at < count:
        tiles.append((at, count - at))
    return tiles


def unfold(plan, src, x_ref):
    fold, block = plan.fold, plan.sources * SUB
    for q in range(fold.groups):
        lo = q * fold.padded
        x_ref[q * block : (q + 1) * block, :] = src[:, lo : lo + fold.width]
    at = fold.groups * block
    for p, lo, hi in fold.spans():
        rows = jnp.dot(
            tail_pick(fold, plan.sources, p),
            src[:, fold.tail_at : fold.tail_at + (hi - lo)],
            preferred_element_type=jnp.float32,
        )
        x_ref[at : at + plan.sources * fold.rest, lo:hi] = rows.astype(jnp.bfloat16)


def refold(plan, o_ref, dst):
    fold, block = plan.fold, plan.sources * SUB
    for q in range(fold.groups):
        lo = q * fold.padded
        dst[:, lo : lo + fold.width] = o_ref[q * block : (q + 1) * block, :]
    at = fold.groups * block
    total = None
    for p, lo, hi in fold.spans():
        rows = lax.dot_general(
            tail_pick(fold, plan.sources, p),
            o_ref[at : at + plan.sources * fold.rest, lo:hi],
            (((0,), (0,)), ((), ())),
            preferred_element_type=jnp.float32,
        )
        if hi - lo < fold.piece:
            blank = jnp.zeros((rows.shape[0], fold.piece - (hi - lo)), jnp.float32)
            rows = jnp.concatenate([rows, blank], axis=1)
        total = rows if total is None else total + rows
    if total is not None:
        dst[:, fold.tail_at :] = total.astype(jnp.bfloat16)


def expert_kernel(plan, up_tiles, down_tiles, *refs):
    refs = list(refs)
    n = plan.parts

    def take(count):
        taken = refs[:count]
        del refs[:count]
        return taken

    if up_tiles:
        in_refs = take(n)
        hbm = take(2)
    else:
        (h_ref,) = take(1)
        hbm = []
    if down_tiles:
        hbm = hbm + take(1)
        out_refs = take(n)
    else:
        (h_ref,) = take(1)
    (stage_ref,) = take(1)
    if up_tiles:
        (x_ref,) = take(1)
    if up_tiles and down_tiles:
        (h_ref,) = take(1)
    if down_tiles:
        (o_ref,) = take(1)
    sems = refs.pop()
    ring, last = refs[: len(hbm)], refs[len(hbm) :]
    down_at = len(hbm) - 1

    def slot(which, tiles, t):
        size = tiles[t][1]
        if t == len(tiles) - 1:
            return last[which]
        ref = ring[which].at[t % DEPTH]
        return ref if size == TILE else ref.at[:, 0:size]

    def copy(which, tiles, t):
        lo, size = tiles[t]
        sem = DEPTH if t == len(tiles) - 1 else t % DEPTH
        return pltpu.make_async_copy(
            hbm[which].at[0, :, lo : lo + size], slot(which, tiles, t), sems.at[which, sem]
        )

    jobs = [[copy(0, up_tiles, t), copy(1, up_tiles, t)] for t in range(len(up_tiles))]
    jobs += [[copy(down_at, down_tiles, t)] for t in range(len(down_tiles))]

    for job in jobs[:DEPTH]:
        for c in job:
            c.start()
    if up_tiles:
        plan.gather(in_refs, stage_ref)
        unfold(plan, stage_ref, x_ref)

    for j, job in enumerate(jobs):
        for c in job:
            c.wait()
        if j < len(up_tiles):
            lo, size = up_tiles[j]
            gate = jnp.dot(x_ref[...], slot(0, up_tiles, j)[...], preferred_element_type=jnp.float32)
            up = jnp.dot(x_ref[...], slot(1, up_tiles, j)[...], preferred_element_type=jnp.float32)
            hidden = (up + 1.0) * gate * jax.nn.sigmoid(alpha_glu * gate)
            h_ref[:, lo : lo + size] = hidden.astype(jnp.bfloat16)
        else:
            t = j - len(up_tiles)
            lo, size = down_tiles[t]
            weights = slot(down_at, down_tiles, t)[...]
            made = jnp.dot(h_ref[...], weights, preferred_element_type=jnp.float32)
            o_ref[:, lo : lo + size] = made.astype(jnp.bfloat16)
        if j + DEPTH < len(jobs):
            for c in jobs[j + DEPTH]:
                c.start()
    if down_tiles:
        refold(plan, o_ref, stage_ref)
        plan.scatter(stage_ref, out_refs)


def vmem_params(limit):
    return pltpu.CompilerParams(vmem_limit_bytes=limit)


def run_experts(plan, rows_in, up_weights, down_weight, limit):
    width, ff = plan.fold.width, plan.ff
    up_tiles = column_tiles(ff) if up_weights else []
    down_tiles = column_tiles(width) if down_weight is not None else []
    rows = plan.sources * plan.fold.slots
    here = pl.BlockSpec(memory_space=pltpu.VMEM)
    there = pl.BlockSpec(memory_space=pltpu.HBM)
    vmem = lambda *shape: pltpu.VMEM(shape, jnp.bfloat16)
    weights = list(up_weights) + ([down_weight] if down_tiles else [])
    if down_tiles:
        out_shape = [plan.part_shape] * plan.parts
    else:
        out_shape = [jax.ShapeDtypeStruct((rows, ff), jnp.bfloat16)]
    scratch = [plan.stage]
    if up_tiles:
        scratch.append(vmem(rows, width))
    if up_tiles and down_tiles:
        scratch.append(vmem(rows, ff))
    if down_tiles:
        scratch.append(vmem(rows, width))
    rings, lasts = [], []
    for tiles, depth in [(up_tiles, width)] * len(up_weights) + [(down_tiles, ff)] * bool(down_tiles):
        rings.append(vmem(DEPTH, depth, TILE))
        lasts.append(vmem(depth, tiles[-1][1]))
    scratch += rings + lasts + [pltpu.SemaphoreType.DMA((len(weights), DEPTH + 1))]
    return pl.pallas_call(
        functools.partial(expert_kernel, plan, up_tiles, down_tiles),
        out_shape=out_shape,
        in_specs=[here] * len(rows_in) + [there] * len(weights),
        out_specs=[here] * len(out_shape),
        scratch_shapes=scratch,
        compiler_params=vmem_params(limit),
        cost_estimate=pl.CostEstimate(
            flops=2 * len(weights) * rows * width * ff,
            bytes_accessed=2 * len(weights) * width * ff,
            transcendentals=rows * ff if up_tiles else 0,
        ),
    )(*rows_in, *weights)


def body(tokens, expert_ids, route_weights, w_gate, w_up, w_down):
    site_count = lax.axis_size("site")
    members = lax.axis_size("member")
    experts = EXP_SITE * site_count
    tok_count, width = tokens.shape
    top_count = expert_ids.shape[1]
    mean_rows = tok_count * top_count // experts
    most_rows = mean_rows + max(1, mean_rows // 8)
    half = site_count // 2
    plan = Plan(half, members, experts // 2, Fold(most_rows, width), w_gate.shape[2])
    sources = plan.sources

    swap = [(s, (s + half) % site_count) for s in range(site_count)]
    halves = [list(range(h * sources, (h + 1) * sources)) for h in range(2)]

    def exchange(parts):
        if not plan.pairwise:
            return [
                lax.all_to_all(
                    parts[0], ("site", "member"), split_axis=0, concat_axis=0, tiled=True,
                    axis_index_groups=halves,
                )
            ]
        return [parts[0]] + [
            lax.ppermute(parts[k], ("site", "member"), [(i, i ^ k) for i in range(2 * sources)])
            for k in range(1, sources)
        ]

    small = vmem_params(SMALL if plan.pairwise else LARGE)
    parts_shape = [plan.part_shape] * plan.parts
    rows_shape = jax.ShapeDtypeStruct(tokens.shape, tokens.dtype)
    route_shape = jax.ShapeDtypeStruct((2 * top_count, tok_count), jnp.float32)

    def call(kernel, out_shape):
        return pl.pallas_call(
            functools.partial(kernel, plan),
            out_shape=out_shape,
            scratch_shapes=[plan.stage],
            compiler_params=small,
        )

    limit = MIDDLE if plan.pairwise else LARGE

    far_tokens = lax.ppermute(tokens, "site", swap)
    *own_packed, route = call(own_pack_kernel, parts_shape + [route_shape])(
        expert_ids.T, route_weights.T, tokens
    )
    far_route = lax.ppermute(route, "site", swap)
    own_in = exchange(own_packed)
    far_packed = call(far_pack_kernel, parts_shape)(far_route, far_tokens)
    far_in = exchange(far_packed)
    own_hidden = run_experts(plan, own_in, (w_gate, w_up), None, limit)
    far_made = run_experts(plan, far_in, (w_gate, w_up), w_down, limit)
    far_back = exchange(far_made)
    own_made = run_experts(plan, own_hidden, (), w_down, limit)
    far_sum = call(held_kernel, rows_shape)(far_route, *far_back)
    other = lax.ppermute(far_sum, "site", [(b, a) for a, b in swap])
    own_back = exchange(own_made)
    return call(final_kernel, rows_shape)(route, other, *own_back)


def solution(mesh):
    placed = (
        P(("groups", "site", "member"), None),
        P(("groups", "site", "member"), None),
        P(("groups", "site", "member"), None),
        P(("site", "member"), None, None),
        P(("site", "member"), None, None),
        P(("site", "member"), None, None),
    )
    return jax.shard_map(
        body,
        mesh=mesh,
        in_specs=placed,
        out_specs=P(("groups", "site", "member"), None),
        check_vma=False,
    )
```

time: 234 us -> 112 us (0.48)
  the two profiles are of different devices: /device:TPU:11 before, /device:TPU:0 now
where the time goes in v2:
time: 112 us
  Pallas kernels  40.9 us (37%)
  waiting for transfers between devices  34.8 us (31%)
  starting transfers between devices  33.6 us (30%)
  local copies, waits for them, and re-layouts  2.38 us (2%)
    pallas_call x3, Pallas kernels, run_experts(): pl.pallas_call(functools.partial(expert_kernel, plan, up_tiles, down_tile...  37.7 us
    ppermute x28, starting transfers between devices, exchange(): lax.ppermute(parts[k], ('site', 'member'), [(i, i ^ k) for i in range(2 *...  26.1 us
    ppermute x28, waiting for transfers between devices, exchange(): lax.ppermute(parts[k], ('site', 'member'), [(i, i ^ k) for i in range(2 *...  20.6 us
    ppermute x1, waiting for transfers between devices, body(): far_route = lax.ppermute(route, 'site', swap)  14.2 us
    ppermute x1, starting transfers between devices, body(): far_tokens = lax.ppermute(tokens, 'site', swap)  4.06 us
    ppermute x1, starting transfers between devices, body(): other = lax.ppermute(far_sum, 'site', [(b, a) for a, b in swap])  3.41 us
    unnamed x6, local copies, waits for them, and re-layouts  2.38 us
  transfers between devices with their start and end apart: 31, of which 12 were waited for; matrix products, arithmetic and copies ran while one was open for 0% of the time, Pallas kernels for 34%

profile of v2, /device:TPU:0, one launch (start us, length us, event | category | flops | bytes accessed | tf_op | source)
XLA Modules:
  0.0 111.9 jit_solution(18300332951877197248)
XLA Ops:
  0.0 4.1 %collective-permute-start.1 = (bf16[64,2880]{1,0:T(8,128)(2,1)}, bf16[64,2880]{1,0:T(8,128)(2,1)S(1)}, u32[]{:S(2)}, u32[]{:S(2)}) collective-permute-start(bf16[64,2880]{1,0:T(8,128)(2,1)} %tokens_ref.1), channel_id=1, source_target_pairs={{0,8},{4,12},{8,0},{12,4},{1,9},{5,13},{9,1},{13,5},{2,10},{6,14},... | collective-permute-start | bytes 1105928 | tf_op jit(solution)/shard_map/ppermute | solution.py:416
  4.1 1.0 copy-done
  5.1 0.7 copy-done.1
  5.8 0.7 copy-done.2
  6.5 0.6 shard_map.64
  7.1 14.2 %collective-permute-done.route_ref = f32[8,64]{1,0:T(8,128)S(1)} collective-permute-done((f32[8,64]{1,0:T(8,128)S(1)}, f32[8,64]{1,0:T(8,128)S(1)}, u32[]{:S(2)}, u32[]{:S(2)}) %collective-permute-start) | collective-permute-done | bytes 2080 | tf_op jit(solution)/shard_map/ppermute | solution.py:420
  21.3 0.6 shard_map.65
  22.0 1.6 %collective-permute-start.3 = (bf16[8,6656]{1,0:T(8,128)(2,1)S(1)}, bf16[8,6656]{1,0:T(8,128)(2,1)S(1)}, u32[]{:S(2)}, u32[]{:S(2)}) collective-permute-start(bf16[8,6656]{1,0:T(8,128)(2,1)S(1)} %get-tuple-element.41), channel_id=1, source_target_pairs={{0,2},{1,3},{2,0},{3,1},{4,6},{5,7},{6,4},{7,5},{8,10},{9,11},{10,... | collective-permute-start | bytes 319496 | tf_op jit(solution)/shard_map/ppermute | solution.py:397
  23.8 0.8 collective-permute-start.5
  24.6 0.9 collective-permute-start.6
  25.5 1.7 %collective-permute-start.7 = (bf16[8,6656]{1,0:T(8,128)(2,1)S(1)}, bf16[8,6656]{1,0:T(8,128)(2,1)S(1)}, u32[]{:S(2)}, u32[]{:S(2)}) collective-permute-start(bf16[8,6656]{1,0:T(8,128)(2,1)S(1)} %get-tuple-element.45), channel_id=1, source_target_pairs={{0,6},{1,7},{2,4},{3,5},{4,2},{5,3},{6,0},{7,1},{8,14},{9,15},{10,... | collective-permute-start | bytes 319496 | tf_op jit(solution)/shard_map/ppermute | solution.py:397
  27.2 0.6 collective-permute-done.3.refs_2_
  27.9 0.4 collective-permute-start.8
  28.2 0.8 collective-permute-done.4.refs_3_
  29.1 0.7 collective-permute-start.17
  29.7 1.6 %collective-permute-start.18 = (bf16[8,6656]{1,0:T(8,128)(2,1)S(1)}, bf16[8,6656]{1,0:T(8,128)(2,1)S(1)}, u32[]{:S(2)}, u32[]{:S(2)}) collective-permute-start(bf16[8,6656]{1,0:T(8,128)(2,1)S(1)} %get-tuple-element.57), channel_id=1, source_target_pairs={{0,2},{1,3},{2,0},{3,1},{4,6},{5,7},{6,4},{7,5},{8,10},{9,11},{10,... | collective-permute-start | bytes 319496 | tf_op jit(solution)/shard_map/ppermute | solution.py:397
  31.3 1.9 %collective-permute-start.19 = (bf16[8,6656]{1,0:T(8,128)(2,1)S(1)}, bf16[8,6656]{1,0:T(8,128)(2,1)S(1)}, u32[]{:S(2)}, u32[]{:S(2)}) collective-permute-start(bf16[8,6656]{1,0:T(8,128)(2,1)S(1)} %get-tuple-element.58), channel_id=1, source_target_pairs={{0,3},{1,2},{2,1},{3,0},{4,7},{5,6},{6,5},{7,4},{8,11},{9,10},{10,... | collective-permute-start | bytes 319496 | tf_op jit(solution)/shard_map/ppermute | solution.py:397
  33.2 2.1 %collective-permute-done.7.refs_6_ = bf16[8,6656]{1,0:T(8,128)(2,1)S(1)} collective-permute-done((bf16[8,6656]{1,0:T(8,128)(2,1)S(1)}, bf16[8,6656]{1,0:T(8,128)(2,1)S(1)}, u32[]{:S(2)}, u32[]{:S(2)}) %collective-permute-start.7) | collective-permute-done | bytes 106528 | tf_op jit(solution)/shard_map/ppermute | solution.py:397
  35.3 0.7 collective-permute-start.20
  36.4 1.0 collective-permute-start.21
  37.3 18.2 %shard_map.66 = (bf16[8,6656]{1,0:T(8,128)(2,1)S(1)}, bf16[8,6656]{1,0:T(8,128)(2,1)S(1)}, bf16[8,6656]{1,0:T(8,128)(2,1)S(1)}, bf16[8,6656]{1,0:T(8,128)(2,1)S(...) custom-call(bf16[8,6656]{1,0:T(8,128)(2,1)S(1)} %get-tuple-element.3, ...), custom_call_target="tpu_custom_call" | custom-call | flops 7166361600 | bytes 49766400 | tf_op jit(solution)/shard_map/pallas_call | solution.py:358
  55.5 1.1 collective-permute-start.22
  56.6 1.4 %collective-permute-start.23 = (bf16[8,6656]{1,0:T(8,128)(2,1)S(1)}, bf16[8,6656]{1,0:T(8,128)(2,1)S(1)}, u32[]{:S(2)}, u32[]{:S(2)}) collective-permute-start(bf16[8,6656]{1,0:T(8,128)(2,1)S(1)} %get-tuple-element.62), channel_id=1, source_target_pairs={{0,7},{1,6},{2,5},{3,4},{4,3},{5,2},{6,1},{7,0},{8,15},{9,14},{10,... | collective-permute-start | bytes 319496 | tf_op jit(solution)/shard_map/ppermute | solution.py:397
  58.0 0.7 collective-permute-start.9
  58.6 0.3 collective-permute-start.10
  59.0 1.1 collective-permute-start.11
  60.0 2.4 %collective-permute-done.22.refs_6_ = bf16[8,6656]{1,0:T(8,128)(2,1)S(1)} collective-permute-done((bf16[8,6656]{1,0:T(8,128)(2,1)S(1)}, bf16[8,6656]{1,0:T(8,128)(2,1)S(1)}, u32[]{:S(2)}, u32[]{:S(2)}) %collective-permute-start.22) | collective-permute-done | bytes 106528 | tf_op jit(solution)/shard_map/ppermute | solution.py:397
  62.4 1.4 %collective-permute-start.12 = (bf16[8,6656]{1,0:T(8,128)(2,1)S(1)}, bf16[8,6656]{1,0:T(8,128)(2,1)S(1)}, u32[]{:S(2)}, u32[]{:S(2)}) collective-permute-start(bf16[8,6656]{1,0:T(8,128)(2,1)S(1)} %get-tuple-element.51), channel_id=1, source_target_pairs={{0,4},{1,5},{2,6},{3,7},{4,0},{5,1},{6,2},{7,3},{8,12},{9,13},{10,... | collective-permute-start | bytes 319496 | tf_op jit(solution)/shard_map/ppermute | solution.py:397
  63.8 0.9 collective-permute-start.13
  64.7 0.5 collective-permute-start.14
  65.2 0.9 collective-permute-done.10.refs_2_
  66.1 0.7 collective-permute-start.15
  66.8 12.4 %shard_map.68.refs_0_ = bf16[144,2880]{1,0:T(8,128)(2,1)S(1)} custom-call(bf16[8,6656]{1,0:T(8,128)(2,1)S(1)} %get-tuple-element.55.refs_0_, bf16[8,6656]{1,0:T(8,128)(2,1)S(1)} %collective-permute-done.17.refs_1_, bf16[8,6656]{1,0:T(8,128)(2,1)S(1)} %collective-permute-done.18.refs_2_, bf16[8,6656]{1,0:T(8,128)(2,1)S(1)} %collective-permute-done.19.refs_3_, ...), custom_call_target="tpu_custom_call" | custom-call | flops 4777574400 | bytes 33177600 | tf_op jit(solution)/shard_map/pallas_call | solution.py:358
  79.3 0.6 shard_map.67
  80.0 3.4 %collective-permute-start.16 = (bf16[64,2880]{1,0:T(8,128)(2,1)S(1)}, bf16[64,2880]{1,0:T(8,128)(2,1)S(1)}, u32[]{:S(2)}, u32[]{:S(2)}) collective-permute-start(bf16[64,2880]{1,0:T(8,128)(2,1)S(1)} %shard_map.67), channel_id=1, source_target_pairs={{8,0},{12,4},{0,8},{4,12},{9,1},{13,5},{1,9},{5,13},{10,2},{14,6},... | collective-permute-start | bytes 1105928 | tf_op jit(solution)/shard_map/ppermute | solution.py:429
  83.4 7.1 %shard_map.69 = (bf16[8,6656]{1,0:T(8,128)(2,1)S(1)}, bf16[8,6656]{1,0:T(8,128)(2,1)S(1)}, bf16[8,6656]{1,0:T(8,128)(2,1)S(1)}, bf16[8,6656]{1,0:T(8,128)(2,1)S(...) custom-call(bf16[144,2880]{1,0:T(8,128)(2,1)S(1)} %shard_map.68.refs, ...), custom_call_target="tpu_custom_call" | custom-call | flops 2388787200 | bytes 16588800 | tf_op jit(solution)/shard_map/pallas_call | solution.py:358
  90.6 1.3 %collective-permute-start.25 = (bf16[8,6656]{1,0:T(8,128)(2,1)S(1)}, bf16[8,6656]{1,0:T(8,128)(2,1)S(1)}, u32[]{:S(2)}, u32[]{:S(2)}) collective-permute-start(bf16[8,6656]{1,0:T(8,128)(2,1)S(1)} %get-tuple-element.65), channel_id=1, source_target_pairs={{0,2},{1,3},{2,0},{3,1},{4,6},{5,7},{6,4},{7,5},{8,10},{9,11},{10,... | collective-permute-start | bytes 319496 | tf_op jit(solution)/shard_map/ppermute | solution.py:397
  91.8 0.6 collective-permute-start.26
  92.4 0.9 collective-permute-start.27
  93.3 0.8 collective-permute-start.28
  94.1 2.3 %collective-permute-done.25.refs_2_ = bf16[8,6656]{1,0:T(8,128)(2,1)S(1)} collective-permute-done((bf16[8,6656]{1,0:T(8,128)(2,1)S(1)}, bf16[8,6656]{1,0:T(8,128)(2,1)S(1)}, u32[]{:S(2)}, u32[]{:S(2)}) %collective-permute-start.25) | collective-permute-done | bytes 106528 | tf_op jit(solution)/shard_map/ppermute | solution.py:397
  96.5 1.7 %collective-permute-start.29 = (bf16[8,6656]{1,0:T(8,128)(2,1)S(1)}, bf16[8,6656]{1,0:T(8,128)(2,1)S(1)}, u32[]{:S(2)}, u32[]{:S(2)}) collective-permute-start(bf16[8,6656]{1,0:T(8,128)(2,1)S(1)} %get-tuple-element.69), channel_id=1, source_target_pairs={{0,6},{1,7},{2,4},{3,5},{4,2},{5,3},{6,0},{7,1},{8,14},{9,15},{10,... | collective-permute-start | bytes 319496 | tf_op jit(solution)/shard_map/ppermute | solution.py:397
  98.2 1.3 %collective-permute-start.30 = (bf16[8,6656]{1,0:T(8,128)(2,1)S(1)}, bf16[8,6656]{1,0:T(8,128)(2,1)S(1)}, u32[]{:S(2)}, u32[]{:S(2)}) collective-permute-start(bf16[8,6656]{1,0:T(8,128)(2,1)S(1)} %get-tuple-element.70), channel_id=1, source_target_pairs={{0,7},{1,6},{2,5},{3,4},{4,3},{5,2},{6,1},{7,0},{8,15},{9,14},{10,... | collective-permute-start | bytes 319496 | tf_op jit(solution)/shard_map/ppermute | solution.py:397
  99.5 3.5 %collective-permute-done.27.refs_4_ = bf16[8,6656]{1,0:T(8,128)(2,1)S(1)} collective-permute-done((bf16[8,6656]{1,0:T(8,128)(2,1)S(1)}, bf16[8,6656]{1,0:T(8,128)(2,1)S(1)}, u32[]{:S(2)}, u32[]{:S(2)}) %collective-permute-start.27) | collective-permute-done | bytes 106528 | tf_op jit(solution)/shard_map/ppermute | solution.py:397
  103.0 2.2 %collective-permute-done.28.refs_5_ = bf16[8,6656]{1,0:T(8,128)(2,1)S(1)} collective-permute-done((bf16[8,6656]{1,0:T(8,128)(2,1)S(1)}, bf16[8,6656]{1,0:T(8,128)(2,1)S(1)}, u32[]{:S(2)}, u32[]{:S(2)}) %collective-permute-start.28) | collective-permute-done | bytes 106528 | tf_op jit(solution)/shard_map/ppermute | solution.py:397
  105.1 3.1 %collective-permute-done.29.refs_6_ = bf16[8,6656]{1,0:T(8,128)(2,1)S(1)} collective-permute-done((bf16[8,6656]{1,0:T(8,128)(2,1)S(1)}, bf16[8,6656]{1,0:T(8,128)(2,1)S(1)}, u32[]{:S(2)}, u32[]{:S(2)}) %collective-permute-start.29) | collective-permute-done | bytes 106528 | tf_op jit(solution)/shard_map/ppermute | solution.py:397
  108.3 2.2 %collective-permute-done.30.refs_7_ = bf16[8,6656]{1,0:T(8,128)(2,1)S(1)} collective-permute-done((bf16[8,6656]{1,0:T(8,128)(2,1)S(1)}, bf16[8,6656]{1,0:T(8,128)(2,1)S(1)}, u32[]{:S(2)}, u32[]{:S(2)}) %collective-permute-start.30) | collective-permute-done | bytes 106528 | tf_op jit(solution)/shard_map/ppermute | solution.py:397
  110.5 1.4 %shard_map.70 = bf16[64,2880]{1,0:T(8,128)(2,1)} custom-call(f32[8,64]{1,0:T(8,128)S(1)} %get-tuple-element.38.route_ref, bf16[64,2880]{1,0:T(8,128)(2,1)S(1)} %collective-permute-done.16.other_ref, bf16[8,6656]{1,0:T(8,128)(2,1)S(1)} %get-tuple-element.63.refs_0_, bf16[8,6656]{1,0:T(8,128)(2,1)S(1)} %collective-permute-done.24.refs_1_, ...), custom_call_target="tpu_custom_call" | custom-call | tf_op jit(solution)/shard_map/pallas_call | solution.py:431
  (27 shorter events, 0.8 us)
Async XLA Ops:
  0.0 21.3 %collective-permute-start.1 = (bf16[64,2880]{1,0:T(8,128)(2,1)}, bf16[64,2880]{1,0:T(8,128)(2,1)S(1)}, u32[]{:S(2)}, u32[]{:S(2)}) collective-permute-start(bf16[64,2880]{1,0:T(8,128)(2,1)} %tokens_ref.1), channel_id=1, source_target_pairs={{0,8},{4,12},{8,0},{12,4},{1,9},{5,13},{9,1},{13,5},{2,10},{6,14},... | collective-permute-start | bytes 1105928 | tf_op jit(solution)/shard_map/ppermute | solution.py:416
  4.1 1.0 copy-start
  5.1 0.7 copy-start.1
  5.8 0.7 copy-start.2
  7.1 14.2 %collective-permute-start = (f32[8,64]{1,0:T(8,128)S(1)}, f32[8,64]{1,0:T(8,128)S(1)}, u32[]{:S(2)}, u32[]{:S(2)}) collective-permute-start(f32[8,64]{1,0:T(8,128)S(1)} %get-tuple-element.38.route_ref), channel_id=1, source_target_pairs={{0,8},{4,12},{8,0},{12,4},{1,9},{5,13},{9,1},{13,5},{2,10},{6,14},... | collective-permute-start | bytes 6152 | tf_op jit(solution)/shard_map/ppermute | solution.py:420
  21.9 3.6 %collective-permute-start.2 = (bf16[8,6656]{1,0:T(8,128)(2,1)S(1)}, bf16[8,6656]{1,0:T(8,128)(2,1)S(1)}, u32[]{:S(2)}, u32[]{:S(2)}) collective-permute-start(bf16[8,6656]{1,0:T(8,128)(2,1)S(1)} %get-tuple-element.40), channel_id=1, source_target_pairs={{0,1},{1,0},{2,3},{3,2},{4,5},{5,4},{6,7},{7,6},{8,9},{9,8},{10,11... | collective-permute-start | bytes 319496 | tf_op jit(solution)/shard_map/ppermute | solution.py:397
  22.0 5.9 %collective-permute-start.3 = (bf16[8,6656]{1,0:T(8,128)(2,1)S(1)}, bf16[8,6656]{1,0:T(8,128)(2,1)S(1)}, u32[]{:S(2)}, u32[]{:S(2)}) collective-permute-start(bf16[8,6656]{1,0:T(8,128)(2,1)S(1)} %get-tuple-element.41), channel_id=1, source_target_pairs={{0,2},{1,3},{2,0},{3,1},{4,6},{5,7},{6,4},{7,5},{8,10},{9,11},{10,... | collective-permute-start | bytes 319496 | tf_op jit(solution)/shard_map/ppermute | solution.py:397
  23.6 5.5 %collective-permute-start.4 = (bf16[8,6656]{1,0:T(8,128)(2,1)S(1)}, bf16[8,6656]{1,0:T(8,128)(2,1)S(1)}, u32[]{:S(2)}, u32[]{:S(2)}) collective-permute-start(bf16[8,6656]{1,0:T(8,128)(2,1)S(1)} %get-tuple-element.42), channel_id=1, source_target_pairs={{0,3},{1,2},{2,1},{3,0},{4,7},{5,6},{6,5},{7,4},{8,11},{9,10},{10,... | collective-permute-start | bytes 319496 | tf_op jit(solution)/shard_map/ppermute | solution.py:397
  23.8 5.9 %collective-permute-start.5 = (bf16[8,6656]{1,0:T(8,128)(2,1)S(1)}, bf16[8,6656]{1,0:T(8,128)(2,1)S(1)}, u32[]{:S(2)}, u32[]{:S(2)}) collective-permute-start(bf16[8,6656]{1,0:T(8,128)(2,1)S(1)} %get-tuple-element.43), channel_id=1, source_target_pairs={{0,4},{1,5},{2,6},{3,7},{4,0},{5,1},{6,2},{7,3},{8,12},{9,13},{10,... | collective-permute-start | bytes 319496 | tf_op jit(solution)/shard_map/ppermute | solution.py:397
  24.6 6.7 %collective-permute-start.6 = (bf16[8,6656]{1,0:T(8,128)(2,1)S(1)}, bf16[8,6656]{1,0:T(8,128)(2,1)S(1)}, u32[]{:S(2)}, u32[]{:S(2)}) collective-permute-start(bf16[8,6656]{1,0:T(8,128)(2,1)S(1)} %get-tuple-element.44), channel_id=1, source_target_pairs={{0,5},{1,4},{2,7},{3,6},{4,1},{5,0},{6,3},{7,2},{8,13},{9,12},{10,... | collective-permute-start | bytes 319496 | tf_op jit(solution)/shard_map/ppermute | solution.py:397
  25.5 9.8 %collective-permute-start.7 = (bf16[8,6656]{1,0:T(8,128)(2,1)S(1)}, bf16[8,6656]{1,0:T(8,128)(2,1)S(1)}, u32[]{:S(2)}, u32[]{:S(2)}) collective-permute-start(bf16[8,6656]{1,0:T(8,128)(2,1)S(1)} %get-tuple-element.45), channel_id=1, source_target_pairs={{0,6},{1,7},{2,4},{3,5},{4,2},{5,3},{6,0},{7,1},{8,14},{9,15},{10,... | collective-permute-start | bytes 319496 | tf_op jit(solution)/shard_map/ppermute | solution.py:397
  27.9 8.5 %collective-permute-start.8 = (bf16[8,6656]{1,0:T(8,128)(2,1)S(1)}, bf16[8,6656]{1,0:T(8,128)(2,1)S(1)}, u32[]{:S(2)}, u32[]{:S(2)}) collective-permute-start(bf16[8,6656]{1,0:T(8,128)(2,1)S(1)} %get-tuple-element.46), channel_id=1, source_target_pairs={{0,7},{1,6},{2,5},{3,4},{4,3},{5,2},{6,1},{7,0},{8,15},{9,14},{10,... | collective-permute-start | bytes 319496 | tf_op jit(solution)/shard_map/ppermute | solution.py:397
  29.1 26.4 %collective-permute-start.17 = (bf16[8,6656]{1,0:T(8,128)(2,1)S(1)}, bf16[8,6656]{1,0:T(8,128)(2,1)S(1)}, u32[]{:S(2)}, u32[]{:S(2)}) collective-permute-start(bf16[8,6656]{1,0:T(8,128)(2,1)S(1)} %get-tuple-element.56), channel_id=1, source_target_pairs={{0,1},{1,0},{2,3},{3,2},{4,5},{5,4},{6,7},{7,6},{8,9},{9,8},{10,11... | collective-permute-start | bytes 319496 | tf_op jit(solution)/shard_map/ppermute | solution.py:397
  29.7 26.8 %collective-permute-start.18 = (bf16[8,6656]{1,0:T(8,128)(2,1)S(1)}, bf16[8,6656]{1,0:T(8,128)(2,1)S(1)}, u32[]{:S(2)}, u32[]{:S(2)}) collective-permute-start(bf16[8,6656]{1,0:T(8,128)(2,1)S(1)} %get-tuple-element.57), channel_id=1, source_target_pairs={{0,2},{1,3},{2,0},{3,1},{4,6},{5,7},{6,4},{7,5},{8,10},{9,11},{10,... | collective-permute-start | bytes 319496 | tf_op jit(solution)/shard_map/ppermute | solution.py:397
  31.3 26.7 %collective-permute-start.19 = (bf16[8,6656]{1,0:T(8,128)(2,1)S(1)}, bf16[8,6656]{1,0:T(8,128)(2,1)S(1)}, u32[]{:S(2)}, u32[]{:S(2)}) collective-permute-start(bf16[8,6656]{1,0:T(8,128)(2,1)S(1)} %get-tuple-element.58), channel_id=1, source_target_pairs={{0,3},{1,2},{2,1},{3,0},{4,7},{5,6},{6,5},{7,4},{8,11},{9,10},{10,... | collective-permute-start | bytes 319496 | tf_op jit(solution)/shard_map/ppermute | solution.py:397
  35.3 23.3 %collective-permute-start.20 = (bf16[8,6656]{1,0:T(8,128)(2,1)S(1)}, bf16[8,6656]{1,0:T(8,128)(2,1)S(1)}, u32[]{:S(2)}, u32[]{:S(2)}) collective-permute-start(bf16[8,6656]{1,0:T(8,128)(2,1)S(1)} %get-tuple-element.59), channel_id=1, source_target_pairs={{0,4},{1,5},{2,6},{3,7},{4,0},{5,1},{6,2},{7,3},{8,12},{9,13},{10,... | collective-permute-start | bytes 319496 | tf_op jit(solution)/shard_map/ppermute | solution.py:397
  36.4 22.6 %collective-permute-start.21 = (bf16[8,6656]{1,0:T(8,128)(2,1)S(1)}, bf16[8,6656]{1,0:T(8,128)(2,1)S(1)}, u32[]{:S(2)}, u32[]{:S(2)}) collective-permute-start(bf16[8,6656]{1,0:T(8,128)(2,1)S(1)} %get-tuple-element.60), channel_id=1, source_target_pairs={{0,5},{1,4},{2,7},{3,6},{4,1},{5,0},{6,3},{7,2},{8,13},{9,12},{10,... | collective-permute-start | bytes 319496 | tf_op jit(solution)/shard_map/ppermute | solution.py:397
  55.5 6.9 %collective-permute-start.22 = (bf16[8,6656]{1,0:T(8,128)(2,1)S(1)}, bf16[8,6656]{1,0:T(8,128)(2,1)S(1)}, u32[]{:S(2)}, u32[]{:S(2)}) collective-permute-start(bf16[8,6656]{1,0:T(8,128)(2,1)S(1)} %get-tuple-element.61), channel_id=1, source_target_pairs={{0,6},{1,7},{2,4},{3,5},{4,2},{5,3},{6,0},{7,1},{8,14},{9,15},{10,... | collective-permute-start | bytes 319496 | tf_op jit(solution)/shard_map/ppermute | solution.py:397
  56.6 7.2 %collective-permute-start.23 = (bf16[8,6656]{1,0:T(8,128)(2,1)S(1)}, bf16[8,6656]{1,0:T(8,128)(2,1)S(1)}, u32[]{:S(2)}, u32[]{:S(2)}) collective-permute-start(bf16[8,6656]{1,0:T(8,128)(2,1)S(1)} %get-tuple-element.62), channel_id=1, source_target_pairs={{0,7},{1,6},{2,5},{3,4},{4,3},{5,2},{6,1},{7,0},{8,15},{9,14},{10,... | collective-permute-start | bytes 319496 | tf_op jit(solution)/shard_map/ppermute | solution.py:397
  58.0 6.8 %collective-permute-start.9 = (bf16[8,6656]{1,0:T(8,128)(2,1)S(1)}, bf16[8,6656]{1,0:T(8,128)(2,1)S(1)}, u32[]{:S(2)}, u32[]{:S(2)}) collective-permute-start(bf16[8,6656]{1,0:T(8,128)(2,1)S(1)} %get-tuple-element.48), channel_id=1, source_target_pairs={{0,1},{1,0},{2,3},{3,2},{4,5},{5,4},{6,7},{7,6},{8,9},{9,8},{10,11... | collective-permute-start | bytes 319496 | tf_op jit(solution)/shard_map/ppermute | solution.py:397
  58.6 7.5 %collective-permute-start.10 = (bf16[8,6656]{1,0:T(8,128)(2,1)S(1)}, bf16[8,6656]{1,0:T(8,128)(2,1)S(1)}, u32[]{:S(2)}, u32[]{:S(2)}) collective-permute-start(bf16[8,6656]{1,0:T(8,128)(2,1)S(1)} %get-tuple-element.49), channel_id=1, source_target_pairs={{0,2},{1,3},{2,0},{3,1},{4,6},{5,7},{6,4},{7,5},{8,10},{9,11},{10,... | collective-permute-start | bytes 319496 | tf_op jit(solution)/shard_map/ppermute | solution.py:397
  59.0 20.3 %collective-permute-start.11 = (bf16[8,6656]{1,0:T(8,128)(2,1)S(1)}, bf16[8,6656]{1,0:T(8,128)(2,1)S(1)}, u32[]{:S(2)}, u32[]{:S(2)}) collective-permute-start(bf16[8,6656]{1,0:T(8,128)(2,1)S(1)} %get-tuple-element.50), channel_id=1, source_target_pairs={{0,3},{1,2},{2,1},{3,0},{4,7},{5,6},{6,5},{7,4},{8,11},{9,10},{10,... | collective-permute-start | bytes 319496 | tf_op jit(solution)/shard_map/ppermute | solution.py:397
  62.4 16.9 %collective-permute-start.12 = (bf16[8,6656]{1,0:T(8,128)(2,1)S(1)}, bf16[8,6656]{1,0:T(8,128)(2,1)S(1)}, u32[]{:S(2)}, u32[]{:S(2)}) collective-permute-start(bf16[8,6656]{1,0:T(8,128)(2,1)S(1)} %get-tuple-element.51), channel_id=1, source_target_pairs={{0,4},{1,5},{2,6},{3,7},{4,0},{5,1},{6,2},{7,3},{8,12},{9,13},{10,... | collective-permute-start | bytes 319496 | tf_op jit(solution)/shard_map/ppermute | solution.py:397
  63.8 15.5 %collective-permute-start.13 = (bf16[8,6656]{1,0:T(8,128)(2,1)S(1)}, bf16[8,6656]{1,0:T(8,128)(2,1)S(1)}, u32[]{:S(2)}, u32[]{:S(2)}) collective-permute-start(bf16[8,6656]{1,0:T(8,128)(2,1)S(1)} %get-tuple-element.52), channel_id=1, source_target_pairs={{0,5},{1,4},{2,7},{3,6},{4,1},{5,0},{6,3},{7,2},{8,13},{9,12},{10,... | collective-permute-start | bytes 319496 | tf_op jit(solution)/shard_map/ppermute | solution.py:397
  64.7 14.6 %collective-permute-start.14 = (bf16[8,6656]{1,0:T(8,128)(2,1)S(1)}, bf16[8,6656]{1,0:T(8,128)(2,1)S(1)}, u32[]{:S(2)}, u32[]{:S(2)}) collective-permute-start(bf16[8,6656]{1,0:T(8,128)(2,1)S(1)} %get-tuple-element.53), channel_id=1, source_target_pairs={{0,6},{1,7},{2,4},{3,5},{4,2},{5,3},{6,0},{7,1},{8,14},{9,15},{10,... | collective-permute-start | bytes 319496 | tf_op jit(solution)/shard_map/ppermute | solution.py:397
  66.1 13.2 %collective-permute-start.15 = (bf16[8,6656]{1,0:T(8,128)(2,1)S(1)}, bf16[8,6656]{1,0:T(8,128)(2,1)S(1)}, u32[]{:S(2)}, u32[]{:S(2)}) collective-permute-start(bf16[8,6656]{1,0:T(8,128)(2,1)S(1)} %get-tuple-element.54), channel_id=1, source_target_pairs={{0,7},{1,6},{2,5},{3,4},{4,3},{5,2},{6,1},{7,0},{8,15},{9,14},{10,... | collective-permute-start | bytes 319496 | tf_op jit(solution)/shard_map/ppermute | solution.py:397
  80.0 30.5 %collective-permute-start.16 = (bf16[64,2880]{1,0:T(8,128)(2,1)S(1)}, bf16[64,2880]{1,0:T(8,128)(2,1)S(1)}, u32[]{:S(2)}, u32[]{:S(2)}) collective-permute-start(bf16[64,2880]{1,0:T(8,128)(2,1)S(1)} %shard_map.67), channel_id=1, source_target_pairs={{8,0},{12,4},{0,8},{4,12},{9,1},{13,5},{1,9},{5,13},{10,2},{14,6},... | collective-permute-start | bytes 1105928 | tf_op jit(solution)/shard_map/ppermute | solution.py:429
  90.5 2.8 %collective-permute-start.24 = (bf16[8,6656]{1,0:T(8,128)(2,1)S(1)}, bf16[8,6656]{1,0:T(8,128)(2,1)S(1)}, u32[]{:S(2)}, u32[]{:S(2)}) collective-permute-start(bf16[8,6656]{1,0:T(8,128)(2,1)S(1)} %get-tuple-element.64), channel_id=1, source_target_pairs={{0,1},{1,0},{2,3},{3,2},{4,5},{5,4},{6,7},{7,6},{8,9},{9,8},{10,11... | collective-permute-start | bytes 319496 | tf_op jit(solution)/shard_map/ppermute | solution.py:397
  90.6 5.9 %collective-permute-start.25 = (bf16[8,6656]{1,0:T(8,128)(2,1)S(1)}, bf16[8,6656]{1,0:T(8,128)(2,1)S(1)}, u32[]{:S(2)}, u32[]{:S(2)}) collective-permute-start(bf16[8,6656]{1,0:T(8,128)(2,1)S(1)} %get-tuple-element.65), channel_id=1, source_target_pairs={{0,2},{1,3},{2,0},{3,1},{4,6},{5,7},{6,4},{7,5},{8,10},{9,11},{10,... | collective-permute-start | bytes 319496 | tf_op jit(solution)/shard_map/ppermute | solution.py:397
  91.8 6.4 %collective-permute-start.26 = (bf16[8,6656]{1,0:T(8,128)(2,1)S(1)}, bf16[8,6656]{1,0:T(8,128)(2,1)S(1)}, u32[]{:S(2)}, u32[]{:S(2)}) collective-permute-start(bf16[8,6656]{1,0:T(8,128)(2,1)S(1)} %get-tuple-element.66), channel_id=1, source_target_pairs={{0,3},{1,2},{2,1},{3,0},{4,7},{5,6},{6,5},{7,4},{8,11},{9,10},{10,... | collective-permute-start | bytes 319496 | tf_op jit(solution)/shard_map/ppermute | solution.py:397
  92.4 10.5 %collective-permute-start.27 = (bf16[8,6656]{1,0:T(8,128)(2,1)S(1)}, bf16[8,6656]{1,0:T(8,128)(2,1)S(1)}, u32[]{:S(2)}, u32[]{:S(2)}) collective-permute-start(bf16[8,6656]{1,0:T(8,128)(2,1)S(1)} %get-tuple-element.67), channel_id=1, source_target_pairs={{0,4},{1,5},{2,6},{3,7},{4,0},{5,1},{6,2},{7,3},{8,12},{9,13},{10,... | collective-permute-start | bytes 319496 | tf_op jit(solution)/shard_map/ppermute | solution.py:397
  93.3 11.8 %collective-permute-start.28 = (bf16[8,6656]{1,0:T(8,128)(2,1)S(1)}, bf16[8,6656]{1,0:T(8,128)(2,1)S(1)}, u32[]{:S(2)}, u32[]{:S(2)}) collective-permute-start(bf16[8,6656]{1,0:T(8,128)(2,1)S(1)} %get-tuple-element.68), channel_id=1, source_target_pairs={{0,5},{1,4},{2,7},{3,6},{4,1},{5,0},{6,3},{7,2},{8,13},{9,12},{10,... | collective-permute-start | bytes 319496 | tf_op jit(solution)/shard_map/ppermute | solution.py:397
  96.5 11.8 %collective-permute-start.29 = (bf16[8,6656]{1,0:T(8,128)(2,1)S(1)}, bf16[8,6656]{1,0:T(8,128)(2,1)S(1)}, u32[]{:S(2)}, u32[]{:S(2)}) collective-permute-start(bf16[8,6656]{1,0:T(8,128)(2,1)S(1)} %get-tuple-element.69), channel_id=1, source_target_pairs={{0,6},{1,7},{2,4},{3,5},{4,2},{5,3},{6,0},{7,1},{8,14},{9,15},{10,... | collective-permute-start | bytes 319496 | tf_op jit(solution)/shard_map/ppermute | solution.py:397
  98.2 12.2 %collective-permute-start.30 = (bf16[8,6656]{1,0:T(8,128)(2,1)S(1)}, bf16[8,6656]{1,0:T(8,128)(2,1)S(1)}, u32[]{:S(2)}, u32[]{:S(2)}) collective-permute-start(bf16[8,6656]{1,0:T(8,128)(2,1)S(1)} %get-tuple-element.70), channel_id=1, source_target_pairs={{0,7},{1,6},{2,5},{3,4},{4,3},{5,2},{6,1},{7,0},{8,15},{9,14},{10,... | collective-permute-start | bytes 319496 | tf_op jit(solution)/shard_map/ppermute | solution.py:397

commit v3 on v2

--- a/solution.py
+++ b/solution.py
@@ -13,8 +13,7 @@
 TILE = 512
 DEPTH = 3
 MOST_PERMUTES = 8
-SMALL = 12 << 20
-MIDDLE = 44 << 20
+MIDDLE = 18 << 20
 LARGE = 60 * 1024 * 1024
 
 alpha_glu = 1.702
@@ -55,6 +54,7 @@
         self.fold = fold
         self.ff = ff
         self.parts = self.sources if self.pairwise else 1
+        self.resident = self.pairwise
         self.part_rows = self.sources * SUB // self.parts
 
     def expert_of(self, chunk):
@@ -257,12 +257,15 @@
         del refs[:count]
         return taken
 
+    hbm, resident = [], []
     if up_tiles:
         in_refs = take(n)
-        hbm = take(2)
+        if plan.resident:
+            resident = [take(len(up_tiles)), take(len(up_tiles))]
+        else:
+            hbm = take(2)
     else:
         (h_ref,) = take(1)
-        hbm = []
     if down_tiles:
         hbm = hbm + take(1)
         out_refs = take(n)
@@ -275,9 +278,10 @@
         (h_ref,) = take(1)
     if down_tiles:
         (o_ref,) = take(1)
-    sems = refs.pop()
+    sems = refs.pop() if hbm else None
     ring, last = refs[: len(hbm)], refs[len(hbm) :]
     down_at = len(hbm) - 1
+    ahead = len(up_tiles) + DEPTH if resident else DEPTH
 
     def slot(which, tiles, t):
         size = tiles[t][1]
@@ -293,10 +297,13 @@
             hbm[which].at[0, :, lo : lo + size], slot(which, tiles, t), sems.at[which, sem]
         )
 
-    jobs = [[copy(0, up_tiles, t), copy(1, up_tiles, t)] for t in range(len(up_tiles))]
+    jobs = [
+        [] if resident else [copy(0, up_tiles, t), copy(1, up_tiles, t)]
+        for t in range(len(up_tiles))
+    ]
     jobs += [[copy(down_at, down_tiles, t)] for t in range(len(down_tiles))]
 
-    for job in jobs[:DEPTH]:
+    for job in jobs[:ahead]:
         for c in job:
             c.start()
     if up_tiles:
@@ -308,8 +315,9 @@
             c.wait()
         if j < len(up_tiles):
             lo, size = up_tiles[j]
-            gate = jnp.dot(x_ref[...], slot(0, up_tiles, j)[...], preferred_element_type=jnp.float32)
-            up = jnp.dot(x_ref[...], slot(1, up_tiles, j)[...], preferred_element_type=jnp.float32)
+            pair = [m[j] for m in resident] or [slot(0, up_tiles, j), slot(1, up_tiles, j)]
+            gate = jnp.dot(x_ref[...], pair[0][...], preferred_element_type=jnp.float32)
+            up = jnp.dot(x_ref[...], pair[1][...], preferred_element_type=jnp.float32)
             hidden = (up + 1.0) * gate * jax.nn.sigmoid(alpha_glu * gate)
             h_ref[:, lo : lo + size] = hidden.astype(jnp.bfloat16)
         else:
@@ -318,12 +326,44 @@
             weights = slot(down_at, down_tiles, t)[...]
             made = jnp.dot(h_ref[...], weights, preferred_element_type=jnp.float32)
             o_ref[:, lo : lo + size] = made.astype(jnp.bfloat16)
-        if j + DEPTH < len(jobs):
-            for c in jobs[j + DEPTH]:
+        if not resident or j >= len(up_tiles):
+            for c in jobs[j + DEPTH] if j + DEPTH < len(jobs) else []:
                 c.start()
     if down_tiles:
         refold(plan, o_ref, stage_ref)
         plan.scatter(stage_ref, out_refs)
+
+
+def load_kernel(tiles, count, *refs):
+    hbm, held, sems = refs[:count], refs[count:-1], refs[-1]
+    copies = [
+        pltpu.make_async_copy(
+            ref.at[0, :, lo : lo + size], held[m * len(tiles) + t], sems.at[m, t]
+        )
+        for t, (lo, size) in enumerate(tiles)
+        for m, ref in enumerate(hbm)
+    ]
+    for c in copies:
+        c.start()
+    for c in copies:
+        c.wait()
+
+
+def load_weights(weights):
+    depth = weights[0].shape[1]
+    tiles = column_tiles(weights[0].shape[2])
+    return pl.pallas_call(
+        functools.partial(load_kernel, tiles, len(weights)),
+        out_shape=[pltpu.VMEM((depth, size), jnp.bfloat16) for _ in weights for _, size in tiles],
+        in_specs=[pl.BlockSpec(memory_space=pltpu.HBM)] * len(weights),
+        out_specs=[pl.BlockSpec(memory_space=pltpu.VMEM)] * (len(weights) * len(tiles)),
+        scratch_shapes=[pltpu.SemaphoreType.DMA((len(weights), len(tiles)))],
+        name="load",
+        compiler_params=vmem_params(MIDDLE),
+        cost_estimate=pl.CostEstimate(
+            flops=0, bytes_accessed=2 * sum(w.size for w in weights), transcendentals=0
+        ),
+    )(*[pltpu.with_memory_space_constraint(w, pltpu.HBM) for w in weights])
 
 
 def vmem_params(limit):
@@ -338,7 +378,9 @@
     here = pl.BlockSpec(memory_space=pltpu.VMEM)
     there = pl.BlockSpec(memory_space=pltpu.HBM)
     vmem = lambda *shape: pltpu.VMEM(shape, jnp.bfloat16)
-    weights = list(up_weights) + ([down_weight] if down_tiles else [])
+    held = list(up_weights) if plan.resident else []
+    streamed = [] if plan.resident else list(up_weights)
+    weights = streamed + ([down_weight] if down_tiles else [])
     if down_tiles:
         out_shape = [plan.part_shape] * plan.parts
     else:
@@ -351,23 +393,26 @@
     if down_tiles:
         scratch.append(vmem(rows, width))
     rings, lasts = [], []
-    for tiles, depth in [(up_tiles, width)] * len(up_weights) + [(down_tiles, ff)] * bool(down_tiles):
+    for tiles, depth in [(up_tiles, width)] * len(streamed) + [(down_tiles, ff)] * bool(down_tiles):
         rings.append(vmem(DEPTH, depth, TILE))
         lasts.append(vmem(depth, tiles[-1][1]))
-    scratch += rings + lasts + [pltpu.SemaphoreType.DMA((len(weights), DEPTH + 1))]
+    scratch += rings + lasts
+    if weights:
+        scratch.append(pltpu.SemaphoreType.DMA((len(weights), DEPTH + 1)))
+    products = (2 if up_tiles else 0) + (1 if down_tiles else 0)
     return pl.pallas_call(
         functools.partial(expert_kernel, plan, up_tiles, down_tiles),
         out_shape=out_shape,
-        in_specs=[here] * len(rows_in) + [there] * len(weights),
+        in_specs=[here] * (len(rows_in) + len(held)) + [there] * len(weights),
         out_specs=[here] * len(out_shape),
         scratch_shapes=scratch,
         compiler_params=vmem_params(limit),
         cost_estimate=pl.CostEstimate(
-            flops=2 * len(weights) * rows * width * ff,
-            bytes_accessed=2 * len(weights) * width * ff,
+            flops=2 * products * rows * width * ff,
+            bytes_accessed=2 * products * width * ff,
             transcendentals=rows * ff if up_tiles else 0,
         ),
-    )(*rows_in, *weights)
+    )(*rows_in, *held, *[pltpu.with_memory_space_constraint(w, pltpu.HBM) for w in weights])
 
 
 def body(tokens, expert_ids, route_weights, w_gate, w_up, w_down):
@@ -398,7 +443,7 @@
             for k in range(1, sources)
         ]
 
-    small = vmem_params(SMALL if plan.pairwise else LARGE)
+    small = vmem_params(MIDDLE if plan.pairwise else LARGE)
     parts_shape = [plan.part_shape] * plan.parts
     rows_shape = jax.ShapeDtypeStruct(tokens.shape, tokens.dtype)
     route_shape = jax.ShapeDtypeStruct((2 * top_count, tok_count), jnp.float32)
@@ -419,10 +464,11 @@
     )
     far_route = lax.ppermute(route, "site", swap)
     own_in = exchange(own_packed)
+    up_weights = load_weights((w_gate, w_up)) if plan.resident else (w_gate, w_up)
     far_packed = call(far_pack_kernel, parts_shape)(far_route, far_tokens)
     far_in = exchange(far_packed)
-    own_hidden = run_experts(plan, own_in, (w_gate, w_up), None, limit)
-    far_made = run_experts(plan, far_in, (w_gate, w_up), w_down, limit)
+    own_hidden = run_experts(plan, own_in, up_weights, None, limit)
+    far_made = run_experts(plan, far_in, up_weights, w_down, limit)
     far_back = exchange(far_made)
     own_made = run_experts(plan, own_hidden, (), w_down, limit)
     far_sum = call(held_kernel, rows_shape)(far_route, *far_back)

time: 112 us -> 107 us (0.955)
  waiting for transfers between devices: 34.8 us -> 31.1 us
  Pallas kernels: 40.9 us -> 39.4 us
    pallas_call x3, Pallas kernels: 37.7 us -> 25.1 us  [run_experts(): pl.pallas_call(functools.partial(expert_kernel, plan, up_tiles, down_tile...]
    pallas_call x0 -> x1, Pallas kernels: none -> 11.1 us  [load_weights(): pl.pallas_call(functools.partial(load_kernel, tiles, len(weights)), out_s...]
    ppermute x28, waiting for transfers between devices: 20.6 us -> 16.9 us  [exchange(): lax.ppermute(parts[k], ('site', 'member'), [(i, i ^ k) for i in range(2 *...]
  transfers between devices with their start and end apart: 31 -> 31, of which waited for: 12 -> 10; matrix products, arithmetic and copies ran while one was open for 0% -> 0% of each run, Pallas kernels for 34% -> 34%
where the time goes in v3:
time: 107 us
  Pallas kernels  39.4 us (37%)
  starting transfers between devices  34 us (32%)
  waiting for transfers between devices  31.1 us (29%)
  local copies, waits for them, and re-layouts  2.38 us (2%)
    ppermute x28, starting transfers between devices, exchange(): lax.ppermute(parts[k], ('site', 'member'), [(i, i ^ k) for i in range(2 *...  26.9 us
    pallas_call x3, Pallas kernels, run_experts(): pl.pallas_call(functools.partial(expert_kernel, plan, up_tiles, down_tile...  25.1 us
    ppermute x28, waiting for transfers between devices, exchange(): lax.ppermute(parts[k], ('site', 'member'), [(i, i ^ k) for i in range(2 *...  16.9 us
    ppermute x1, waiting for transfers between devices, body(): far_route = lax.ppermute(route, 'site', swap)  14.2 us
    pallas_call x1, Pallas kernels, load_weights(): pl.pallas_call(functools.partial(load_kernel, tiles, len(weights)), out_s...  11.1 us
    ppermute x1, starting transfers between devices, body(): far_tokens = lax.ppermute(tokens, 'site', swap)  4.06 us
    ppermute x1, starting transfers between devices, body(): other = lax.ppermute(far_sum, 'site', [(b, a) for a, b in swap])  2.91 us
    unnamed x6, local copies, waits for them, and re-layouts  2.38 us
  transfers between devices with their start and end apart: 31, of which 10 were waited for; matrix products, arithmetic and copies ran while one was open for 0% of the time, Pallas kernels for 34%

profile of v3, /device:TPU:0, one launch (start us, length us, event | category | flops | bytes accessed | tf_op | source)
XLA Modules:
  0.0 107.0 jit_solution(18178968125417801543)
XLA Ops:
  0.0 4.1 %collective-permute-start.1 = (bf16[64,2880]{1,0:T(8,128)(2,1)}, bf16[64,2880]{1,0:T(8,128)(2,1)S(1)}, u32[]{:S(2)}, u32[]{:S(2)}) collective-permute-start(bf16[64,2880]{1,0:T(8,128)(2,1)} %tokens_ref.1), channel_id=1, source_target_pairs={{0,8},{4,12},{8,0},{12,4},{1,9},{5,13},{9,1},{13,5},{2,10},{6,14},... | collective-permute-start | bytes 1105928 | tf_op jit(solution)/shard_map/ppermute | solution.py:461
  4.1 1.0 copy-done
  5.1 0.7 copy-done.1
  5.8 0.7 copy-done.2
  6.5 0.6 shard_map.64
  7.1 14.2 %collective-permute-done.route_ref = f32[8,64]{1,0:T(8,128)S(1)} collective-permute-done((f32[8,64]{1,0:T(8,128)S(1)}, f32[8,64]{1,0:T(8,128)S(1)}, u32[]{:S(2)}, u32[]{:S(2)}) %collective-permute-start) | collective-permute-done | bytes 2080 | tf_op jit(solution)/shard_map/ppermute | solution.py:465
  21.3 0.6 shard_map.65
  22.0 1.6 %collective-permute-start.3 = (bf16[8,6656]{1,0:T(8,128)(2,1)S(1)}, bf16[8,6656]{1,0:T(8,128)(2,1)S(1)}, u32[]{:S(2)}, u32[]{:S(2)}) collective-permute-start(bf16[8,6656]{1,0:T(8,128)(2,1)S(1)} %get-tuple-element.55), channel_id=1, source_target_pairs={{0,2},{1,3},{2,0},{3,1},{4,6},{5,7},{6,4},{7,5},{8,10},{9,11},{10,... | collective-permute-start | bytes 319496 | tf_op jit(solution)/shard_map/ppermute | solution.py:442
  23.8 0.8 collective-permute-start.5
  24.6 0.9 collective-permute-start.6
  25.5 1.7 %collective-permute-start.7 = (bf16[8,6656]{1,0:T(8,128)(2,1)S(1)}, bf16[8,6656]{1,0:T(8,128)(2,1)S(1)}, u32[]{:S(2)}, u32[]{:S(2)}) collective-permute-start(bf16[8,6656]{1,0:T(8,128)(2,1)S(1)} %get-tuple-element.59), channel_id=1, source_target_pairs={{0,6},{1,7},{2,4},{3,5},{4,2},{5,3},{6,0},{7,1},{8,14},{9,15},{10,... | collective-permute-start | bytes 319496 | tf_op jit(solution)/shard_map/ppermute | solution.py:442
  27.2 0.6 collective-permute-done.3.refs_2_
  27.9 0.4 collective-permute-start.8
  28.2 11.1 %load.1 = (bf16[2880,256]{1,0:T(8,128)(2,1)S(1)}, bf16[2880,256]{1,0:T(8,128)(2,1)S(1)}, bf16[2880,512]{1,0:T(8,128)(2,1)S(1)}, bf16[2880,512]{1,0:T(8,128)(2,1)...) custom-call(bf16[1,2880,2880]{2,1,0:T(8,128)(2,1)} %refs_0_.1, ...), custom_call_target="tpu_custom_call" | custom-call | bytes 33177600 | tf_op jit(solution)/shard_map/load/pallas_call | solution.py:355
  39.3 1.5 %collective-permute-start.17 = (bf16[8,6656]{1,0:T(8,128)(2,1)S(1)}, bf16[8,6656]{1,0:T(8,128)(2,1)S(1)}, u32[]{:S(2)}, u32[]{:S(2)}) collective-permute-start(bf16[8,6656]{1,0:T(8,128)(2,1)S(1)} %get-tuple-element.84), channel_id=1, source_target_pairs={{0,1},{1,0},{2,3},{3,2},{4,5},{5,4},{6,7},{7,6},{8,9},{9,8},{10,11... | collective-permute-start | bytes 319496 | tf_op jit(solution)/shard_map/ppermute | solution.py:442
  40.9 0.5 collective-permute-start.18
  41.4 0.9 collective-permute-start.19
  42.3 1.3 %collective-permute-start.20 = (bf16[8,6656]{1,0:T(8,128)(2,1)S(1)}, bf16[8,6656]{1,0:T(8,128)(2,1)S(1)}, u32[]{:S(2)}, u32[]{:S(2)}) collective-permute-start(bf16[8,6656]{1,0:T(8,128)(2,1)S(1)} %get-tuple-element.87), channel_id=1, source_target_pairs={{0,4},{1,5},{2,6},{3,7},{4,0},{5,1},{6,2},{7,3},{8,12},{9,13},{10,... | collective-permute-start | bytes 319496 | tf_op jit(solution)/shard_map/ppermute | solution.py:442
  43.6 0.8 collective-permute-start.21
  44.4 12.0 %shard_map.66 = (bf16[8,6656]{1,0:T(8,128)(2,1)S(1)}, bf16[8,6656]{1,0:T(8,128)(2,1)S(1)}, bf16[8,6656]{1,0:T(8,128)(2,1)S(1)}, bf16[8,6656]{1,0:T(8,128)(2,1)S(...) custom-call(bf16[8,6656]{1,0:T(8,128)(2,1)S(1)} %get-tuple-element.5, ...), custom_call_target="tpu_custom_call" | custom-call | flops 7166361600 | bytes 49766400 | tf_op jit(solution)/shard_map/pallas_call | solution.py:403
  56.3 1.3 %collective-permute-start.22 = (bf16[8,6656]{1,0:T(8,128)(2,1)S(1)}, bf16[8,6656]{1,0:T(8,128)(2,1)S(1)}, u32[]{:S(2)}, u32[]{:S(2)}) collective-permute-start(bf16[8,6656]{1,0:T(8,128)(2,1)S(1)} %get-tuple-element.89), channel_id=1, source_target_pairs={{0,6},{1,7},{2,4},{3,5},{4,2},{5,3},{6,0},{7,1},{8,14},{9,15},{10,... | collective-permute-start | bytes 319496 | tf_op jit(solution)/shard_map/ppermute | solution.py:442
  57.6 1.1 %collective-permute-start.23 = (bf16[8,6656]{1,0:T(8,128)(2,1)S(1)}, bf16[8,6656]{1,0:T(8,128)(2,1)S(1)}, u32[]{:S(2)}, u32[]{:S(2)}) collective-permute-start(bf16[8,6656]{1,0:T(8,128)(2,1)S(1)} %get-tuple-element.90), channel_id=1, source_target_pairs={{0,7},{1,6},{2,5},{3,4},{4,3},{5,2},{6,1},{7,0},{8,15},{9,14},{10,... | collective-permute-start | bytes 319496 | tf_op jit(solution)/shard_map/ppermute | solution.py:442
  58.8 0.7 collective-permute-start.9
  59.5 0.5 collective-permute-start.10
  60.0 0.9 collective-permute-start.11
  60.9 2.2 %collective-permute-done.22.refs_6_ = bf16[8,6656]{1,0:T(8,128)(2,1)S(1)} collective-permute-done((bf16[8,6656]{1,0:T(8,128)(2,1)S(1)}, bf16[8,6656]{1,0:T(8,128)(2,1)S(1)}, u32[]{:S(2)}, u32[]{:S(2)}) %collective-permute-start.22) | collective-permute-done | bytes 106528 | tf_op jit(solution)/shard_map/ppermute | solution.py:442
  63.1 1.4 %collective-permute-start.12 = (bf16[8,6656]{1,0:T(8,128)(2,1)S(1)}, bf16[8,6656]{1,0:T(8,128)(2,1)S(1)}, u32[]{:S(2)}, u32[]{:S(2)}) collective-permute-start(bf16[8,6656]{1,0:T(8,128)(2,1)S(1)} %get-tuple-element.79), channel_id=1, source_target_pairs={{0,4},{1,5},{2,6},{3,7},{4,0},{5,1},{6,2},{7,3},{8,12},{9,13},{10,... | collective-permute-start | bytes 319496 | tf_op jit(solution)/shard_map/ppermute | solution.py:442
  64.6 1.0 collective-permute-start.13
  65.6 0.9 collective-permute-start.14
  66.5 0.4 collective-permute-done.10.refs_2_
  66.9 0.9 collective-permute-start.15
  67.9 6.1 %shard_map.68.refs_0_ = bf16[144,2880]{1,0:T(8,128)(2,1)S(1)} custom-call(bf16[8,6656]{1,0:T(8,128)(2,1)S(1)} %get-tuple-element.83.refs_0_, bf16[8,6656]{1,0:T(8,128)(2,1)S(1)} %collective-permute-done.17.refs_1_, bf16[8,6656]{1,0:T(8,128)(2,1)S(1)} %collective-permute-done.18.refs_2_, bf16[8,6656]{1,0:T(8,128)(2,1)S(1)} %collective-permute-done.19.refs_3_, ...), custom_call_target="tpu_custom_call" | custom-call | flops 4777574400 | bytes 33177600 | tf_op jit(solution)/shard_map/pallas_call | solution.py:403
  74.0 0.3 collective-permute-done.15.refs_7_
  74.3 0.6 shard_map.67
  75.0 2.9 %collective-permute-start.16 = (bf16[64,2880]{1,0:T(8,128)(2,1)S(1)}, bf16[64,2880]{1,0:T(8,128)(2,1)S(1)}, u32[]{:S(2)}, u32[]{:S(2)}) collective-permute-start(bf16[64,2880]{1,0:T(8,128)(2,1)S(1)} %shard_map.67), channel_id=1, source_target_pairs={{8,0},{12,4},{0,8},{4,12},{9,1},{13,5},{1,9},{5,13},{10,2},{14,6},... | collective-permute-start | bytes 1105928 | tf_op jit(solution)/shard_map/ppermute | solution.py:475
  77.9 7.1 %shard_map.69 = (bf16[8,6656]{1,0:T(8,128)(2,1)S(1)}, bf16[8,6656]{1,0:T(8,128)(2,1)S(1)}, bf16[8,6656]{1,0:T(8,128)(2,1)S(1)}, bf16[8,6656]{1,0:T(8,128)(2,1)S(...) custom-call(bf16[144,2880]{1,0:T(8,128)(2,1)S(1)} %shard_map.68.refs, ...), custom_call_target="tpu_custom_call" | custom-call | flops 2388787200 | bytes 16588800 | tf_op jit(solution)/shard_map/pallas_call | solution.py:403
  85.0 0.5 collective-permute-start.24
  85.5 1.4 %collective-permute-start.25 = (bf16[8,6656]{1,0:T(8,128)(2,1)S(1)}, bf16[8,6656]{1,0:T(8,128)(2,1)S(1)}, u32[]{:S(2)}, u32[]{:S(2)}) collective-permute-start(bf16[8,6656]{1,0:T(8,128)(2,1)S(1)} %get-tuple-element.93), channel_id=1, source_target_pairs={{0,2},{1,3},{2,0},{3,1},{4,6},{5,7},{6,4},{7,5},{8,10},{9,11},{10,... | collective-permute-start | bytes 319496 | tf_op jit(solution)/shard_map/ppermute | solution.py:442
  86.9 1.2 %collective-permute-start.27 = (bf16[8,6656]{1,0:T(8,128)(2,1)S(1)}, bf16[8,6656]{1,0:T(8,128)(2,1)S(1)}, u32[]{:S(2)}, u32[]{:S(2)}) collective-permute-start(bf16[8,6656]{1,0:T(8,128)(2,1)S(1)} %get-tuple-element.95), channel_id=1, source_target_pairs={{0,4},{1,5},{2,6},{3,7},{4,0},{5,1},{6,2},{7,3},{8,12},{9,13},{10,... | collective-permute-start | bytes 319496 | tf_op jit(solution)/shard_map/ppermute | solution.py:442
  88.1 0.9 collective-permute-start.28
  89.0 2.0 %collective-permute-done.25.refs_2_ = bf16[8,6656]{1,0:T(8,128)(2,1)S(1)} collective-permute-done((bf16[8,6656]{1,0:T(8,128)(2,1)S(1)}, bf16[8,6656]{1,0:T(8,128)(2,1)S(1)}, u32[]{:S(2)}, u32[]{:S(2)}) %collective-permute-start.25) | collective-permute-done | bytes 106528 | tf_op jit(solution)/shard_map/ppermute | solution.py:442
  91.0 1.9 %collective-permute-start.29 = (bf16[8,6656]{1,0:T(8,128)(2,1)S(1)}, bf16[8,6656]{1,0:T(8,128)(2,1)S(1)}, u32[]{:S(2)}, u32[]{:S(2)}) collective-permute-start(bf16[8,6656]{1,0:T(8,128)(2,1)S(1)} %get-tuple-element.97), channel_id=1, source_target_pairs={{0,6},{1,7},{2,4},{3,5},{4,2},{5,3},{6,0},{7,1},{8,14},{9,15},{10,... | collective-permute-start | bytes 319496 | tf_op jit(solution)/shard_map/ppermute | solution.py:442
  92.9 1.4 %collective-permute-start.30 = (bf16[8,6656]{1,0:T(8,128)(2,1)S(1)}, bf16[8,6656]{1,0:T(8,128)(2,1)S(1)}, u32[]{:S(2)}, u32[]{:S(2)}) collective-permute-start(bf16[8,6656]{1,0:T(8,128)(2,1)S(1)} %get-tuple-element.98), channel_id=1, source_target_pairs={{0,7},{1,6},{2,5},{3,4},{4,3},{5,2},{6,1},{7,0},{8,15},{9,14},{10,... | collective-permute-start | bytes 319496 | tf_op jit(solution)/shard_map/ppermute | solution.py:442
  94.3 3.6 %collective-permute-done.27.refs_4_ = bf16[8,6656]{1,0:T(8,128)(2,1)S(1)} collective-permute-done((bf16[8,6656]{1,0:T(8,128)(2,1)S(1)}, bf16[8,6656]{1,0:T(8,128)(2,1)S(1)}, u32[]{:S(2)}, u32[]{:S(2)}) %collective-permute-start.27) | collective-permute-done | bytes 106528 | tf_op jit(solution)/shard_map/ppermute | solution.py:442
  97.9 2.2 %collective-permute-done.28.refs_5_ = bf16[8,6656]{1,0:T(8,128)(2,1)S(1)} collective-permute-done((bf16[8,6656]{1,0:T(8,128)(2,1)S(1)}, bf16[8,6656]{1,0:T(8,128)(2,1)S(1)}, u32[]{:S(2)}, u32[]{:S(2)}) %collective-permute-start.28) | collective-permute-done | bytes 106528 | tf_op jit(solution)/shard_map/ppermute | solution.py:442
  100.2 3.2 %collective-permute-done.29.refs_6_ = bf16[8,6656]{1,0:T(8,128)(2,1)S(1)} collective-permute-done((bf16[8,6656]{1,0:T(8,128)(2,1)S(1)}, bf16[8,6656]{1,0:T(8,128)(2,1)S(1)}, u32[]{:S(2)}, u32[]{:S(2)}) %collective-permute-start.29) | collective-permute-done | bytes 106528 | tf_op jit(solution)/shard_map/ppermute | solution.py:442
  103.4 2.2 %collective-permute-done.30.refs_7_ = bf16[8,6656]{1,0:T(8,128)(2,1)S(1)} collective-permute-done((bf16[8,6656]{1,0:T(8,128)(2,1)S(1)}, bf16[8,6656]{1,0:T(8,128)(2,1)S(1)}, u32[]{:S(2)}, u32[]{:S(2)}) %collective-permute-start.30) | collective-permute-done | bytes 106528 | tf_op jit(solution)/shard_map/ppermute | solution.py:442
  105.6 1.4 %shard_map.70 = bf16[64,2880]{1,0:T(8,128)(2,1)} custom-call(f32[8,64]{1,0:T(8,128)S(1)} %get-tuple-element.52.route_ref, bf16[64,2880]{1,0:T(8,128)(2,1)S(1)} %collective-permute-done.16.other_ref, bf16[8,6656]{1,0:T(8,128)(2,1)S(1)} %get-tuple-element.91.refs_0_, bf16[8,6656]{1,0:T(8,128)(2,1)S(1)} %collective-permute-done.24.refs_1_, ...), custom_call_target="tpu_custom_call" | custom-call | tf_op jit(solution)/shard_map/pallas_call | solution.py:477
  (28 shorter events, 0.4 us)
Async XLA Ops:
  0.0 21.3 %collective-permute-start.1 = (bf16[64,2880]{1,0:T(8,128)(2,1)}, bf16[64,2880]{1,0:T(8,128)(2,1)S(1)}, u32[]{:S(2)}, u32[]{:S(2)}) collective-permute-start(bf16[64,2880]{1,0:T(8,128)(2,1)} %tokens_ref.1), channel_id=1, source_target_pairs={{0,8},{4,12},{8,0},{12,4},{1,9},{5,13},{9,1},{13,5},{2,10},{6,14},... | collective-permute-start | bytes 1105928 | tf_op jit(solution)/shard_map/ppermute | solution.py:461
  4.1 1.0 copy-start
  5.1 0.7 copy-start.1
  5.8 0.7 copy-start.2
  7.1 14.2 %collective-permute-start = (f32[8,64]{1,0:T(8,128)S(1)}, f32[8,64]{1,0:T(8,128)S(1)}, u32[]{:S(2)}, u32[]{:S(2)}) collective-permute-start(f32[8,64]{1,0:T(8,128)S(1)} %get-tuple-element.52.route_ref), channel_id=1, source_target_pairs={{0,8},{4,12},{8,0},{12,4},{1,9},{5,13},{9,1},{13,5},{2,10},{6,14},... | collective-permute-start | bytes 6152 | tf_op jit(solution)/shard_map/ppermute | solution.py:465
  21.9 3.6 %collective-permute-start.2 = (bf16[8,6656]{1,0:T(8,128)(2,1)S(1)}, bf16[8,6656]{1,0:T(8,128)(2,1)S(1)}, u32[]{:S(2)}, u32[]{:S(2)}) collective-permute-start(bf16[8,6656]{1,0:T(8,128)(2,1)S(1)} %get-tuple-element.54), channel_id=1, source_target_pairs={{0,1},{1,0},{2,3},{3,2},{4,5},{5,4},{6,7},{7,6},{8,9},{9,8},{10,11... | collective-permute-start | bytes 319496 | tf_op jit(solution)/shard_map/ppermute | solution.py:442
  22.0 5.9 %collective-permute-start.3 = (bf16[8,6656]{1,0:T(8,128)(2,1)S(1)}, bf16[8,6656]{1,0:T(8,128)(2,1)S(1)}, u32[]{:S(2)}, u32[]{:S(2)}) collective-permute-start(bf16[8,6656]{1,0:T(8,128)(2,1)S(1)} %get-tuple-element.55), channel_id=1, source_target_pairs={{0,2},{1,3},{2,0},{3,1},{4,6},{5,7},{6,4},{7,5},{8,10},{9,11},{10,... | collective-permute-start | bytes 319496 | tf_op jit(solution)/shard_map/ppermute | solution.py:442
  23.6 15.7 %collective-permute-start.4 = (bf16[8,6656]{1,0:T(8,128)(2,1)S(1)}, bf16[8,6656]{1,0:T(8,128)(2,1)S(1)}, u32[]{:S(2)}, u32[]{:S(2)}) collective-permute-start(bf16[8,6656]{1,0:T(8,128)(2,1)S(1)} %get-tuple-element.56), channel_id=1, source_target_pairs={{0,3},{1,2},{2,1},{3,0},{4,7},{5,6},{6,5},{7,4},{8,11},{9,10},{10,... | collective-permute-start | bytes 319496 | tf_op jit(solution)/shard_map/ppermute | solution.py:442
  23.8 17.1 %collective-permute-start.5 = (bf16[8,6656]{1,0:T(8,128)(2,1)S(1)}, bf16[8,6656]{1,0:T(8,128)(2,1)S(1)}, u32[]{:S(2)}, u32[]{:S(2)}) collective-permute-start(bf16[8,6656]{1,0:T(8,128)(2,1)S(1)} %get-tuple-element.57), channel_id=1, source_target_pairs={{0,4},{1,5},{2,6},{3,7},{4,0},{5,1},{6,2},{7,3},{8,12},{9,13},{10,... | collective-permute-start | bytes 319496 | tf_op jit(solution)/shard_map/ppermute | solution.py:442
  24.6 16.8 %collective-permute-start.6 = (bf16[8,6656]{1,0:T(8,128)(2,1)S(1)}, bf16[8,6656]{1,0:T(8,128)(2,1)S(1)}, u32[]{:S(2)}, u32[]{:S(2)}) collective-permute-start(bf16[8,6656]{1,0:T(8,128)(2,1)S(1)} %get-tuple-element.58), channel_id=1, source_target_pairs={{0,5},{1,4},{2,7},{3,6},{4,1},{5,0},{6,3},{7,2},{8,13},{9,12},{10,... | collective-permute-start | bytes 319496 | tf_op jit(solution)/shard_map/ppermute | solution.py:442
  25.5 16.8 %collective-permute-start.7 = (bf16[8,6656]{1,0:T(8,128)(2,1)S(1)}, bf16[8,6656]{1,0:T(8,128)(2,1)S(1)}, u32[]{:S(2)}, u32[]{:S(2)}) collective-permute-start(bf16[8,6656]{1,0:T(8,128)(2,1)S(1)} %get-tuple-element.59), channel_id=1, source_target_pairs={{0,6},{1,7},{2,4},{3,5},{4,2},{5,3},{6,0},{7,1},{8,14},{9,15},{10,... | collective-permute-start | bytes 319496 | tf_op jit(solution)/shard_map/ppermute | solution.py:442
  27.9 15.7 %collective-permute-start.8 = (bf16[8,6656]{1,0:T(8,128)(2,1)S(1)}, bf16[8,6656]{1,0:T(8,128)(2,1)S(1)}, u32[]{:S(2)}, u32[]{:S(2)}) collective-permute-start(bf16[8,6656]{1,0:T(8,128)(2,1)S(1)} %get-tuple-element.60), channel_id=1, source_target_pairs={{0,7},{1,6},{2,5},{3,4},{4,3},{5,2},{6,1},{7,0},{8,15},{9,14},{10,... | collective-permute-start | bytes 319496 | tf_op jit(solution)/shard_map/ppermute | solution.py:442
  39.3 17.0 %collective-permute-start.17 = (bf16[8,6656]{1,0:T(8,128)(2,1)S(1)}, bf16[8,6656]{1,0:T(8,128)(2,1)S(1)}, u32[]{:S(2)}, u32[]{:S(2)}) collective-permute-start(bf16[8,6656]{1,0:T(8,128)(2,1)S(1)} %get-tuple-element.84), channel_id=1, source_target_pairs={{0,1},{1,0},{2,3},{3,2},{4,5},{5,4},{6,7},{7,6},{8,9},{9,8},{10,11... | collective-permute-start | bytes 319496 | tf_op jit(solution)/shard_map/ppermute | solution.py:442
  40.9 16.8 %collective-permute-start.18 = (bf16[8,6656]{1,0:T(8,128)(2,1)S(1)}, bf16[8,6656]{1,0:T(8,128)(2,1)S(1)}, u32[]{:S(2)}, u32[]{:S(2)}) collective-permute-start(bf16[8,6656]{1,0:T(8,128)(2,1)S(1)} %get-tuple-element.85), channel_id=1, source_target_pairs={{0,2},{1,3},{2,0},{3,1},{4,6},{5,7},{6,4},{7,5},{8,10},{9,11},{10,... | collective-permute-start | bytes 319496 | tf_op jit(solution)/shard_map/ppermute | solution.py:442
  41.4 17.3 %collective-permute-start.19 = (bf16[8,6656]{1,0:T(8,128)(2,1)S(1)}, bf16[8,6656]{1,0:T(8,128)(2,1)S(1)}, u32[]{:S(2)}, u32[]{:S(2)}) collective-permute-start(bf16[8,6656]{1,0:T(8,128)(2,1)S(1)} %get-tuple-element.86), channel_id=1, source_target_pairs={{0,3},{1,2},{2,1},{3,0},{4,7},{5,6},{6,5},{7,4},{8,11},{9,10},{10,... | collective-permute-start | bytes 319496 | tf_op jit(solution)/shard_map/ppermute | solution.py:442
  42.3 17.1 %collective-permute-start.20 = (bf16[8,6656]{1,0:T(8,128)(2,1)S(1)}, bf16[8,6656]{1,0:T(8,128)(2,1)S(1)}, u32[]{:S(2)}, u32[]{:S(2)}) collective-permute-start(bf16[8,6656]{1,0:T(8,128)(2,1)S(1)} %get-tuple-element.87), channel_id=1, source_target_pairs={{0,4},{1,5},{2,6},{3,7},{4,0},{5,1},{6,2},{7,3},{8,12},{9,13},{10,... | collective-permute-start | bytes 319496 | tf_op jit(solution)/shard_map/ppermute | solution.py:442
  43.6 16.4 %collective-permute-start.21 = (bf16[8,6656]{1,0:T(8,128)(2,1)S(1)}, bf16[8,6656]{1,0:T(8,128)(2,1)S(1)}, u32[]{:S(2)}, u32[]{:S(2)}) collective-permute-start(bf16[8,6656]{1,0:T(8,128)(2,1)S(1)} %get-tuple-element.88), channel_id=1, source_target_pairs={{0,5},{1,4},{2,7},{3,6},{4,1},{5,0},{6,3},{7,2},{8,13},{9,12},{10,... | collective-permute-start | bytes 319496 | tf_op jit(solution)/shard_map/ppermute | solution.py:442
  56.3 6.8 %collective-permute-start.22 = (bf16[8,6656]{1,0:T(8,128)(2,1)S(1)}, bf16[8,6656]{1,0:T(8,128)(2,1)S(1)}, u32[]{:S(2)}, u32[]{:S(2)}) collective-permute-start(bf16[8,6656]{1,0:T(8,128)(2,1)S(1)} %get-tuple-element.89), channel_id=1, source_target_pairs={{0,6},{1,7},{2,4},{3,5},{4,2},{5,3},{6,0},{7,1},{8,14},{9,15},{10,... | collective-permute-start | bytes 319496 | tf_op jit(solution)/shard_map/ppermute | solution.py:442
  57.6 6.9 %collective-permute-start.23 = (bf16[8,6656]{1,0:T(8,128)(2,1)S(1)}, bf16[8,6656]{1,0:T(8,128)(2,1)S(1)}, u32[]{:S(2)}, u32[]{:S(2)}) collective-permute-start(bf16[8,6656]{1,0:T(8,128)(2,1)S(1)} %get-tuple-element.90), channel_id=1, source_target_pairs={{0,7},{1,6},{2,5},{3,4},{4,3},{5,2},{6,1},{7,0},{8,15},{9,14},{10,... | collective-permute-start | bytes 319496 | tf_op jit(solution)/shard_map/ppermute | solution.py:442
  58.8 6.8 %collective-permute-start.9 = (bf16[8,6656]{1,0:T(8,128)(2,1)S(1)}, bf16[8,6656]{1,0:T(8,128)(2,1)S(1)}, u32[]{:S(2)}, u32[]{:S(2)}) collective-permute-start(bf16[8,6656]{1,0:T(8,128)(2,1)S(1)} %get-tuple-element.76), channel_id=1, source_target_pairs={{0,1},{1,0},{2,3},{3,2},{4,5},{5,4},{6,7},{7,6},{8,9},{9,8},{10,11... | collective-permute-start | bytes 319496 | tf_op jit(solution)/shard_map/ppermute | solution.py:442
  59.5 7.4 %collective-permute-start.10 = (bf16[8,6656]{1,0:T(8,128)(2,1)S(1)}, bf16[8,6656]{1,0:T(8,128)(2,1)S(1)}, u32[]{:S(2)}, u32[]{:S(2)}) collective-permute-start(bf16[8,6656]{1,0:T(8,128)(2,1)S(1)} %get-tuple-element.77), channel_id=1, source_target_pairs={{0,2},{1,3},{2,0},{3,1},{4,6},{5,7},{6,4},{7,5},{8,10},{9,11},{10,... | collective-permute-start | bytes 319496 | tf_op jit(solution)/shard_map/ppermute | solution.py:442
  60.0 14.0 %collective-permute-start.11 = (bf16[8,6656]{1,0:T(8,128)(2,1)S(1)}, bf16[8,6656]{1,0:T(8,128)(2,1)S(1)}, u32[]{:S(2)}, u32[]{:S(2)}) collective-permute-start(bf16[8,6656]{1,0:T(8,128)(2,1)S(1)} %get-tuple-element.78), channel_id=1, source_target_pairs={{0,3},{1,2},{2,1},{3,0},{4,7},{5,6},{6,5},{7,4},{8,11},{9,10},{10,... | collective-permute-start | bytes 319496 | tf_op jit(solution)/shard_map/ppermute | solution.py:442
  63.1 10.9 %collective-permute-start.12 = (bf16[8,6656]{1,0:T(8,128)(2,1)S(1)}, bf16[8,6656]{1,0:T(8,128)(2,1)S(1)}, u32[]{:S(2)}, u32[]{:S(2)}) collective-permute-start(bf16[8,6656]{1,0:T(8,128)(2,1)S(1)} %get-tuple-element.79), channel_id=1, source_target_pairs={{0,4},{1,5},{2,6},{3,7},{4,0},{5,1},{6,2},{7,3},{8,12},{9,13},{10,... | collective-permute-start | bytes 319496 | tf_op jit(solution)/shard_map/ppermute | solution.py:442
  64.6 9.4 %collective-permute-start.13 = (bf16[8,6656]{1,0:T(8,128)(2,1)S(1)}, bf16[8,6656]{1,0:T(8,128)(2,1)S(1)}, u32[]{:S(2)}, u32[]{:S(2)}) collective-permute-start(bf16[8,6656]{1,0:T(8,128)(2,1)S(1)} %get-tuple-element.80), channel_id=1, source_target_pairs={{0,5},{1,4},{2,7},{3,6},{4,1},{5,0},{6,3},{7,2},{8,13},{9,12},{10,... | collective-permute-start | bytes 319496 | tf_op jit(solution)/shard_map/ppermute | solution.py:442
  65.6 8.4 %collective-permute-start.14 = (bf16[8,6656]{1,0:T(8,128)(2,1)S(1)}, bf16[8,6656]{1,0:T(8,128)(2,1)S(1)}, u32[]{:S(2)}, u32[]{:S(2)}) collective-permute-start(bf16[8,6656]{1,0:T(8,128)(2,1)S(1)} %get-tuple-element.81), channel_id=1, source_target_pairs={{0,6},{1,7},{2,4},{3,5},{4,2},{5,3},{6,0},{7,1},{8,14},{9,15},{10,... | collective-permute-start | bytes 319496 | tf_op jit(solution)/shard_map/ppermute | solution.py:442
  66.9 7.4 %collective-permute-start.15 = (bf16[8,6656]{1,0:T(8,128)(2,1)S(1)}, bf16[8,6656]{1,0:T(8,128)(2,1)S(1)}, u32[]{:S(2)}, u32[]{:S(2)}) collective-permute-start(bf16[8,6656]{1,0:T(8,128)(2,1)S(1)} %get-tuple-element.82), channel_id=1, source_target_pairs={{0,7},{1,6},{2,5},{3,4},{4,3},{5,2},{6,1},{7,0},{8,15},{9,14},{10,... | collective-permute-start | bytes 319496 | tf_op jit(solution)/shard_map/ppermute | solution.py:442
  75.0 30.6 %collective-permute-start.16 = (bf16[64,2880]{1,0:T(8,128)(2,1)S(1)}, bf16[64,2880]{1,0:T(8,128)(2,1)S(1)}, u32[]{:S(2)}, u32[]{:S(2)}) collective-permute-start(bf16[64,2880]{1,0:T(8,128)(2,1)S(1)} %shard_map.67), channel_id=1, source_target_pairs={{8,0},{12,4},{0,8},{4,12},{9,1},{13,5},{1,9},{5,13},{10,2},{14,6},... | collective-permute-start | bytes 1105928 | tf_op jit(solution)/shard_map/ppermute | solution.py:475
  85.0 3.1 %collective-permute-start.24 = (bf16[8,6656]{1,0:T(8,128)(2,1)S(1)}, bf16[8,6656]{1,0:T(8,128)(2,1)S(1)}, u32[]{:S(2)}, u32[]{:S(2)}) collective-permute-start(bf16[8,6656]{1,0:T(8,128)(2,1)S(1)} %get-tuple-element.92), channel_id=1, source_target_pairs={{0,1},{1,0},{2,3},{3,2},{4,5},{5,4},{6,7},{7,6},{8,9},{9,8},{10,11... | collective-permute-start | bytes 319496 | tf_op jit(solution)/shard_map/ppermute | solution.py:442
  85.5 5.5 %collective-permute-start.25 = (bf16[8,6656]{1,0:T(8,128)(2,1)S(1)}, bf16[8,6656]{1,0:T(8,128)(2,1)S(1)}, u32[]{:S(2)}, u32[]{:S(2)}) collective-permute-start(bf16[8,6656]{1,0:T(8,128)(2,1)S(1)} %get-tuple-element.93), channel_id=1, source_target_pairs={{0,2},{1,3},{2,0},{3,1},{4,6},{5,7},{6,4},{7,5},{8,10},{9,11},{10,... | collective-permute-start | bytes 319496 | tf_op jit(solution)/shard_map/ppermute | solution.py:442
  86.9 6.0 %collective-permute-start.26 = (bf16[8,6656]{1,0:T(8,128)(2,1)S(1)}, bf16[8,6656]{1,0:T(8,128)(2,1)S(1)}, u32[]{:S(2)}, u32[]{:S(2)}) collective-permute-start(bf16[8,6656]{1,0:T(8,128)(2,1)S(1)} %get-tuple-element.94), channel_id=1, source_target_pairs={{0,3},{1,2},{2,1},{3,0},{4,7},{5,6},{6,5},{7,4},{8,11},{9,10},{10,... | collective-permute-start | bytes 319496 | tf_op jit(solution)/shard_map/ppermute | solution.py:442
  86.9 11.0 %collective-permute-start.27 = (bf16[8,6656]{1,0:T(8,128)(2,1)S(1)}, bf16[8,6656]{1,0:T(8,128)(2,1)S(1)}, u32[]{:S(2)}, u32[]{:S(2)}) collective-permute-start(bf16[8,6656]{1,0:T(8,128)(2,1)S(1)} %get-tuple-element.95), channel_id=1, source_target_pairs={{0,4},{1,5},{2,6},{3,7},{4,0},{5,1},{6,2},{7,3},{8,12},{9,13},{10,... | collective-permute-start | bytes 319496 | tf_op jit(solution)/shard_map/ppermute | solution.py:442
  88.1 12.1 %collective-permute-start.28 = (bf16[8,6656]{1,0:T(8,128)(2,1)S(1)}, bf16[8,6656]{1,0:T(8,128)(2,1)S(1)}, u32[]{:S(2)}, u32[]{:S(2)}) collective-permute-start(bf16[8,6656]{1,0:T(8,128)(2,1)S(1)} %get-tuple-element.96), channel_id=1, source_target_pairs={{0,5},{1,4},{2,7},{3,6},{4,1},{5,0},{6,3},{7,2},{8,13},{9,12},{10,... | collective-permute-start | bytes 319496 | tf_op jit(solution)/shard_map/ppermute | solution.py:442
  91.0 12.4 %collective-permute-start.29 = (bf16[8,6656]{1,0:T(8,128)(2,1)S(1)}, bf16[8,6656]{1,0:T(8,128)(2,1)S(1)}, u32[]{:S(2)}, u32[]{:S(2)}) collective-permute-start(bf16[8,6656]{1,0:T(8,128)(2,1)S(1)} %get-tuple-element.97), channel_id=1, source_target_pairs={{0,6},{1,7},{2,4},{3,5},{4,2},{5,3},{6,0},{7,1},{8,14},{9,15},{10,... | collective-permute-start | bytes 319496 | tf_op jit(solution)/shard_map/ppermute | solution.py:442
  92.9 12.7 %collective-permute-start.30 = (bf16[8,6656]{1,0:T(8,128)(2,1)S(1)}, bf16[8,6656]{1,0:T(8,128)(2,1)S(1)}, u32[]{:S(2)}, u32[]{:S(2)}) collective-permute-start(bf16[8,6656]{1,0:T(8,128)(2,1)S(1)} %get-tuple-element.98), channel_id=1, source_target_pairs={{0,7},{1,6},{2,5},{3,4},{4,3},{5,2},{6,1},{7,0},{8,15},{9,14},{10,... | collective-permute-start | bytes 319496 | tf_op jit(solution)/shard_map/ppermute | solution.py:442
